TPU v7x, 128 devices: a whole 4x4x4 slice. The times are simulated.
128 devices in a mesh: section: 16 (over x_hi, z, core), dp: 8 (over y, x_lo).
Axes of the slice: x: 4 (x_hi: 2, x_lo: 2; x = x_hi * 2 + x_lo), y: 4, z: 4, core: 2. Of those that a mesh axis runs over, the one named last changes fastest.
Arguments:
- section_of_layer: int32 [20], replicated, may hold values from 0 to 15, as said below
- lengths: int32 [2, 2, 8], P(None, None, 'dp'), may hold values from 32 to 64, as said below
- layer_gains: float32 [20, 3, 2560], replicated, may hold values from 0.5 to 1.5
- saved_queries: bfloat16 [2, 16, 2, 2, 512, 2560], P(None, 'section', None, None, 'dp'), may hold values from -6 to 6
- saved_keys: bfloat16 [2, 16, 2, 2, 512, 2560], P(None, 'section', None, None, 'dp'), may hold values from -6 to 6
- block_inputs: bfloat16 [2, 16, 2, 512, 2560], P(None, 'section', None, 'dp'), may hold values from -400 to 400
- cotangents: bfloat16 [2, 2, 512, 2560], P(None, None, 'dp'), may hold values from -6 to 6
Outputs:
- input_grads: bfloat16 [2, 16, 2, 512, 2560], P(None, 'section', None, 'dp')
- gain_grads: float32 [16, 2, 3, 2560], P('section')
Inputs may be any that keep to these rules, and one draw needn't show every extreme that they name: `section_of_layer`: never falls; every block holds 1 or 2 layers and some block holds 2; saved slots past a block's layers are unused. `lengths`: some sequence has 64 valid tokens.
All inputs are finite; a program needn't handle non-finite values.
Results may differ from a plain program's by a relative error of at most 0.012.
Values may be sent and summed in bfloat16 or wider, within the bound.
A program may use at most 128 MiB of HBM per device.

v0:
```python
import math

import jax
import jax.numpy as jnp
from jax import lax
from jax.sharding import PartitionSpec as P

HEAD_DIM = 128


norm_epsilon = 1e-06


def from_behind(value, axis, steps):
    count = lax.axis_size(axis)
    initial, last = (max(0, -steps), min(count, count - steps))
    return lax.ppermute(value, axis, [(source, source + steps) for source in range(initial, last)])


def from_partner(block, axis, apart):
    count = lax.axis_size(axis)
    route = []
    for low in range(count):
        high = low | 1 << apart
        if high != low and high < count:
            route += [(low, high), (high, low)]
    return lax.ppermute(block, axis, route)


def split_heads(tensor):
    return tensor.reshape(tensor.shape[0], tensor.shape[1], tensor.shape[2] // HEAD_DIM, HEAD_DIM)


def merge_heads(tensor):
    return tensor.reshape(tensor.shape[0], tensor.shape[1], tensor.shape[2] * tensor.shape[3])


def product(spec, left, right):
    return jnp.einsum(spec, left, right, preferred_element_type=jnp.float32)


def attention_mask(length, seq_len):
    rows_iota = lax.broadcasted_iota(jnp.int32, (seq_len, seq_len), 0)
    cols_iota = lax.broadcasted_iota(jnp.int32, (seq_len, seq_len), 1)
    causal = cols_iota <= rows_iota
    return causal[None, None] & (cols_iota[None, None] < length[:, None, None, None])


def layer_parts(state_in, query_in, key_in, gain_rows, length):
    seq_len = state_in.shape[1]
    score_scale = 1.0 / math.sqrt(HEAD_DIM)
    state_wide = state_in.astype(jnp.float32)
    inv_rms = lax.rsqrt(jnp.mean(state_wide * state_wide, axis=-1, keepdims=True) + norm_epsilon)
    normed = state_wide * inv_rms
    values = (normed * gain_rows[0]).astype(jnp.bfloat16)
    query_scaled = (query_in.astype(jnp.float32) * gain_rows[1]).astype(jnp.bfloat16)
    key_scaled = (key_in.astype(jnp.float32) * gain_rows[2]).astype(jnp.bfloat16)
    scores = (
        product("gihc,gjhc->ghij", split_heads(query_scaled), split_heads(key_scaled)) * score_scale
    )
    allowed = attention_mask(length, seq_len)
    masked = jnp.where(allowed, scores, -1e30)
    row_top = jnp.max(masked, axis=-1, keepdims=True)
    exp_terms = jnp.where(allowed, jnp.exp(masked - row_top), 0.0)
    attn_probs = exp_terms / jnp.sum(exp_terms, axis=-1, keepdims=True)
    return (inv_rms, normed, values, query_scaled, key_scaled, attn_probs)


def layer_forward(state_in, parts):
    mixed_heads = product("ghij,gjhc->gihc", parts[5].astype(jnp.bfloat16), split_heads(parts[2]))
    return (state_in.astype(jnp.float32) + merge_heads(mixed_heads)).astype(jnp.bfloat16)


def layer_backward(grad_out, gain_rows, query_in, key_in, parts):
    inv_rms, normed, values, query_scaled, key_scaled, attn_probs = parts
    score_scale = 1.0 / math.sqrt(HEAD_DIM)
    grad_heads = split_heads(grad_out)
    probs_low = attn_probs.astype(jnp.bfloat16)
    value_grad = merge_heads(product("ghij,gihc->gjhc", probs_low, grad_heads))
    probs_grad = product("gihc,gjhc->ghij", grad_heads, split_heads(values))
    row_delta = jnp.sum(attn_probs * probs_grad, axis=-1, keepdims=True)
    score_grad = (attn_probs * (probs_grad - row_delta) * score_scale).astype(jnp.bfloat16)
    query_grad = merge_heads(product("ghij,gjhc->gihc", score_grad, split_heads(key_scaled)))
    key_grad = merge_heads(product("ghij,gihc->gjhc", score_grad, split_heads(query_scaled)))
    gain_terms = jnp.stack(
        [
            jnp.sum(value_grad * normed, axis=(0, 1)),
            jnp.sum(query_grad * query_in.astype(jnp.float32), axis=(0, 1)),
            jnp.sum(key_grad * key_in.astype(jnp.float32), axis=(0, 1)),
        ]
    )
    normed_grad = value_grad * gain_rows[0]
    state_grad = inv_rms * (
        normed_grad - normed * jnp.mean(normed_grad * normed, axis=-1, keepdims=True)
    )
    return ((grad_out.astype(jnp.float32) + state_grad).astype(jnp.bfloat16), gain_terms)


def block_backward(state_in, query_pair, key_pair, gain_pair, layer_count, grad_out, length):
    first_parts = layer_parts(state_in, query_pair[0], key_pair[0], gain_pair[0], length)

    def two_layers(unused):
        middle = layer_forward(state_in, first_parts)
        second = layer_parts(middle, query_pair[1], key_pair[1], gain_pair[1], length)
        inner_grad, upper_terms = layer_backward(
            grad_out, gain_pair[1], query_pair[1], key_pair[1], second
        )
        outer_grad, lower_terms = layer_backward(
            inner_grad, gain_pair[0], query_pair[0], key_pair[0], first_parts
        )
        return (outer_grad, jnp.stack([lower_terms, upper_terms]))

    def one_layer(unused):
        outer_grad, lower_terms = layer_backward(
            grad_out, gain_pair[0], query_pair[0], key_pair[0], first_parts
        )
        return (outer_grad, jnp.stack([lower_terms, jnp.zeros_like(lower_terms)]))

    return lax.cond(layer_count == 2, two_layers, one_layer, 0)


def block_layers(section_of_layer, block_index, layer_gains):
    layer_count = jnp.sum((section_of_layer == block_index).astype(jnp.int32))
    first_layer = jnp.sum((section_of_layer < block_index).astype(jnp.int32))
    last_layer = layer_gains.shape[0] - 1
    lower_gain = lax.dynamic_index_in_dim(
        layer_gains, jnp.minimum(first_layer, last_layer), 0, keepdims=False
    )
    upper_gain = lax.dynamic_index_in_dim(
        layer_gains, jnp.minimum(first_layer + 1, last_layer), 0, keepdims=False
    )
    return (layer_count, jnp.stack([lower_gain, upper_gain]))


def body(
    section_of_layer, lengths, layer_gains, saved_queries, saved_keys, block_inputs, cotangents
):
    sections = lax.axis_size("section")
    groups = lax.axis_size("dp")
    place_index = lax.axis_index("section")
    micro_count = saved_queries.shape[3]
    seq_len = saved_queries.shape[4]
    feature_count = saved_queries.shape[5]
    tables = (
        block_layers(section_of_layer, place_index, layer_gains),
        block_layers(section_of_layer, sections - 1 - place_index, layer_gains),
    )
    starts = (sections - 1 - place_index, place_index)
    leaders = (place_index == sections - 1, place_index == 0)
    positions = lax.broadcasted_iota(jnp.int32, (seq_len,), 0)

    def run_direction(direction, step_index, incoming, written, totals):
        micro_index = step_index - starts[direction]
        active = (micro_index >= 0) & (micro_index < micro_count)
        chosen = jnp.clip(micro_index, 0, micro_count - 1)
        length = lax.dynamic_index_in_dim(lengths[direction], chosen, 0, keepdims=False)
        seed_grad = lax.dynamic_index_in_dim(cotangents[direction], chosen, 0, keepdims=False)
        seed_grad = jnp.where(
            (positions < length[0])[:, None], seed_grad, jnp.zeros((), jnp.bfloat16)
        )
        grad_out = jnp.where(leaders[direction], seed_grad, incoming)
        state_in = lax.dynamic_index_in_dim(block_inputs[direction, 0], chosen, 0, keepdims=False)
        query_pair = lax.dynamic_index_in_dim(
            saved_queries[direction, 0], chosen, 1, keepdims=False
        )
        key_pair = lax.dynamic_index_in_dim(saved_keys[direction, 0], chosen, 1, keepdims=False)
        layer_count, gain_pair = tables[direction]

        def run_block(unused):
            return block_backward(
                state_in[None],
                query_pair[:, None],
                key_pair[:, None],
                gain_pair,
                layer_count,
                grad_out[None],
                length,
            )

        def skip_block(unused):
            return (
                jnp.zeros((1, seq_len, feature_count), jnp.bfloat16),
                jnp.zeros(gain_pair.shape, jnp.float32),
            )

        block_grad, gain_terms = lax.cond(active, run_block, skip_block, 0)
        block_grad = block_grad[0]
        previous = lax.dynamic_index_in_dim(written, chosen, 0, keepdims=False)
        kept_grad = jnp.where(active, block_grad, previous)
        written = lax.dynamic_update_index_in_dim(written, kept_grad, chosen, 0)
        return (block_grad, written, totals + gain_terms)

    def relay_step(step_index, carry):
        from_above, from_below, written_down, written_up, totals_down, totals_up = carry
        send_down, written_down, totals_down = run_direction(
            0, step_index, from_above, written_down, totals_down
        )
        send_up, written_up, totals_up = run_direction(
            1, step_index, from_below, written_up, totals_up
        )
        from_above = from_behind(send_down, "section", -1)
        from_below = from_behind(send_up, "section", 1)
        return (from_above, from_below, written_down, written_up, totals_down, totals_up)

    zero_grad = jnp.zeros((seq_len, feature_count), jnp.bfloat16)
    zero_written = jnp.zeros((micro_count, seq_len, feature_count), jnp.bfloat16)
    zero_totals = jnp.zeros(tables[0][1].shape, jnp.float32)
    final_carry = lax.fori_loop(
        0,
        sections + micro_count - 1,
        relay_step,
        (zero_grad, zero_grad, zero_written, zero_written, zero_totals, zero_totals),
    )
    written_down, written_up, own_terms, other_terms = (
        final_carry[2],
        final_carry[3],
        final_carry[4],
        final_carry[5],
    )
    input_grads = jnp.stack([written_down, written_up])[:, None]
    mirrored = other_terms
    for bit_index in range(sections.bit_length() - 1):
        mirrored = from_partner(mirrored.astype(jnp.bfloat16), "section", bit_index).astype(
            mirrored.dtype
        )
    own_rows = lax.psum(own_terms + mirrored, "dp")
    gain_grads = (own_rows / groups)[None]
    return (input_grads, gain_grads)


def solution(mesh):
    in_specs = (
        P(),
        P(None, None, "dp"),
        P(),
        P(None, "section", None, None, "dp", None),
        P(None, "section", None, None, "dp", None),
        P(None, "section", None, "dp", None),
        P(None, None, "dp", None),
    )
    out_specs = (P(None, "section", None, "dp", None), P("section", None, None, None))
    return jax.shard_map(body, mesh=mesh, in_specs=in_specs, out_specs=out_specs, check_vma=False)
```

profile of v0, /device:TPU:0, one launch (start us, length us, event | category | flops | bytes accessed | tf_op | source)
XLA Modules:
  0.0 1066.9 jit_solution(1774018521793927973)
XLA Ops:
  12.0 1002.2 %while.25 = (s32[]{:T(128)}, bf16[64,2560]{1,0:T(8,128)(2,1)}, bf16[64,2560]{1,0:T(8,128)(2,1)}, bf16[2,64,2560]{2,1,0:T(8,128)(2,1)}, bf16[2,64,2560]{2,1,0:T(8...) while((s32[]{:T(128)}, bf16[64,2560]{1,0:T(8,128)(2,1)}, ...), condition=%wide.region_53.54_spmd.clone.clone, body=%wide.region_4.53_spmd.clone.clone.sunk | while | flops 491373056 | bytes 250353888 | solution.py:208
  13.2 32.4 %conditional.22 = (bf16[1,64,2560]{2,1,0:T(8,128)(2,1)}, f32[2,3,2560]{2,1,0:T(4,128)}) conditional(s32[]{:T(128)} %convert_element_type.1009, () %tuple.189, (s32[]{:T(128)}, bf16[2,1,2,2,64,2560]{5,4,3,2,1,0:T(8,128)(2,1)}, s32[]{:T(128)}, bf16[2,1,2,2,64,2560]{5,4,3,2,1,0:T(8,128)(2,1)}, pred[]{:T(512)}, /*index=5*/s32[2,2,1]{2,1,0:T(2,128)}, ...), branch_computations={%region_29.29_spmd, %region_30.52_spmd} | conditional | flops 245491968 | bytes 120731728 | solution.py:186
  24.0 1.9 fusion.197
  32.8 10.2 conditional.3
  44.1 1.6 add_convert_fusion.1
  45.7 2.0 collective-permute-start.1
  50.5 2.2 select_dynamic-update-slice_fusion.3
  55.8 32.4 %conditional.22 = (bf16[1,64,2560]{2,1,0:T(8,128)(2,1)}, f32[2,3,2560]{2,1,0:T(4,128)}) conditional(s32[]{:T(128)} %convert_element_type.1009, () %tuple.189, (s32[]{:T(128)}, bf16[2,1,2,2,64,2560]{5,4,3,2,1,0:T(8,128)(2,1)}, s32[]{:T(128)}, bf16[2,1,2,2,64,2560]{5,4,3,2,1,0:T(8,128)(2,1)}, pred[]{:T(512)}, /*index=5*/s32[2,2,1]{2,1,0:T(2,128)}, ...), branch_computations={%region_29.29_spmd, %region_30.52_spmd} | conditional | flops 245491968 | bytes 120731728 | solution.py:186
  66.6 1.9 fusion.197
  75.4 10.2 conditional.3
  86.6 1.6 add_convert_fusion.1
  88.3 3.8 collective-permute-start.1
  94.9 2.2 select_dynamic-update-slice_fusion.3
  101.6 37.1 %collective-permute-start.1 = (bf16[64,2560]{1,0:T(8,128)(2,1)}, bf16[64,2560]{1,0:T(8,128)(2,1)}, u32[]{:S(2)}, u32[]{:S(2)}) collective-permute-start(bf16[64,2560]{1,0:T(8,128)(2,1)} %bitcast.557), channel_id=1, source_target_pairs={{0,8},{8,16},{16,24},{24,32},{32,40},{40,48},{48,56},{56,64},{64,7... | collective-permute-start | bytes 983048 | tf_op jit(solution)/shard_map/while/body/eval_jaxpr/ppermute | solution.py:17
  141.4 2.1 select_dynamic-update-slice_fusion.3
  148.1 6.0 collective-permute-start.1
  156.9 2.1 select_dynamic-update-slice_fusion.3
  160.1 29.1 %collective-permute-done = bf16[64,2560]{1,0:T(8,128)(2,1)S(1)} collective-permute-done((bf16[64,2560]{1,0:T(8,128)(2,1)}, bf16[64,2560]{1,0:T(8,128)(2,1)S(1)}, u32[]{:S(2)}, u32[]{:S(2)}) %collective-permute-start) | collective-permute-done | bytes 327712 | tf_op jit(solution)/shard_map/while/body/eval_jaxpr/ppermute | solution.py:17
  192.6 8.0 collective-permute-start.1
  203.4 2.1 select_dynamic-update-slice_fusion.3
  210.1 32.5 %collective-permute-start.1 = (bf16[64,2560]{1,0:T(8,128)(2,1)}, bf16[64,2560]{1,0:T(8,128)(2,1)}, u32[]{:S(2)}, u32[]{:S(2)}) collective-permute-start(bf16[64,2560]{1,0:T(8,128)(2,1)} %bitcast.557), channel_id=1, source_target_pairs={{0,8},{8,16},{16,24},{24,32},{32,40},{40,48},{48,56},{56,64},{64,7... | collective-permute-start | bytes 983048 | tf_op jit(solution)/shard_map/while/body/eval_jaxpr/ppermute | solution.py:17
  245.4 2.1 select_dynamic-update-slice_fusion.3
  248.6 17.0 %collective-permute-done = bf16[64,2560]{1,0:T(8,128)(2,1)S(1)} collective-permute-done((bf16[64,2560]{1,0:T(8,128)(2,1)}, bf16[64,2560]{1,0:T(8,128)(2,1)S(1)}, u32[]{:S(2)}, u32[]{:S(2)}) %collective-permute-start) | collective-permute-done | bytes 327712 | tf_op jit(solution)/shard_map/while/body/eval_jaxpr/ppermute | solution.py:17
  269.0 11.7 %collective-permute-start.1 = (bf16[64,2560]{1,0:T(8,128)(2,1)}, bf16[64,2560]{1,0:T(8,128)(2,1)}, u32[]{:S(2)}, u32[]{:S(2)}) collective-permute-start(bf16[64,2560]{1,0:T(8,128)(2,1)} %bitcast.557), channel_id=1, source_target_pairs={{0,8},{8,16},{16,24},{24,32},{32,40},{40,48},{48,56},{56,64},{64,7... | collective-permute-start | bytes 983048 | tf_op jit(solution)/shard_map/while/body/eval_jaxpr/ppermute | solution.py:17
  283.5 2.1 select_dynamic-update-slice_fusion.3
  286.6 48.2 %collective-permute-done = bf16[64,2560]{1,0:T(8,128)(2,1)S(1)} collective-permute-done((bf16[64,2560]{1,0:T(8,128)(2,1)}, bf16[64,2560]{1,0:T(8,128)(2,1)S(1)}, u32[]{:S(2)}, u32[]{:S(2)}) %collective-permute-start) | collective-permute-done | bytes 327712 | tf_op jit(solution)/shard_map/while/body/eval_jaxpr/ppermute | solution.py:17
  338.2 11.7 %collective-permute-start.1 = (bf16[64,2560]{1,0:T(8,128)(2,1)}, bf16[64,2560]{1,0:T(8,128)(2,1)}, u32[]{:S(2)}, u32[]{:S(2)}) collective-permute-start(bf16[64,2560]{1,0:T(8,128)(2,1)} %bitcast.557), channel_id=1, source_target_pairs={{0,8},{8,16},{16,24},{24,32},{32,40},{40,48},{48,56},{56,64},{64,7... | collective-permute-start | bytes 983048 | tf_op jit(solution)/shard_map/while/body/eval_jaxpr/ppermute | solution.py:17
  352.7 2.1 select_dynamic-update-slice_fusion.3
  359.3 32.5 %collective-permute-start.1 = (bf16[64,2560]{1,0:T(8,128)(2,1)}, bf16[64,2560]{1,0:T(8,128)(2,1)}, u32[]{:S(2)}, u32[]{:S(2)}) collective-permute-start(bf16[64,2560]{1,0:T(8,128)(2,1)} %bitcast.557), channel_id=1, source_target_pairs={{0,8},{8,16},{16,24},{24,32},{32,40},{40,48},{48,56},{56,64},{64,7... | collective-permute-start | bytes 983048 | tf_op jit(solution)/shard_map/while/body/eval_jaxpr/ppermute | solution.py:17
  394.7 2.1 select_dynamic-update-slice_fusion.3
  401.3 6.0 collective-permute-start.1
  410.2 2.1 select_dynamic-update-slice_fusion.3
  413.3 44.6 %collective-permute-done = bf16[64,2560]{1,0:T(8,128)(2,1)S(1)} collective-permute-done((bf16[64,2560]{1,0:T(8,128)(2,1)}, bf16[64,2560]{1,0:T(8,128)(2,1)S(1)}, u32[]{:S(2)}, u32[]{:S(2)}) %collective-permute-start) | collective-permute-done | bytes 327712 | tf_op jit(solution)/shard_map/while/body/eval_jaxpr/ppermute | solution.py:17
  461.3 15.7 %collective-permute-start.1 = (bf16[64,2560]{1,0:T(8,128)(2,1)}, bf16[64,2560]{1,0:T(8,128)(2,1)}, u32[]{:S(2)}, u32[]{:S(2)}) collective-permute-start(bf16[64,2560]{1,0:T(8,128)(2,1)} %bitcast.557), channel_id=1, source_target_pairs={{0,8},{8,16},{16,24},{24,32},{32,40},{40,48},{48,56},{56,64},{64,7... | collective-permute-start | bytes 983048 | tf_op jit(solution)/shard_map/while/body/eval_jaxpr/ppermute | solution.py:17
  479.8 2.1 select_dynamic-update-slice_fusion.3
  486.4 73.2 %collective-permute-start.1 = (bf16[64,2560]{1,0:T(8,128)(2,1)}, bf16[64,2560]{1,0:T(8,128)(2,1)}, u32[]{:S(2)}, u32[]{:S(2)}) collective-permute-start(bf16[64,2560]{1,0:T(8,128)(2,1)} %bitcast.557), channel_id=1, source_target_pairs={{0,8},{8,16},{16,24},{24,32},{32,40},{40,48},{48,56},{56,64},{64,7... | collective-permute-start | bytes 983048 | tf_op jit(solution)/shard_map/while/body/eval_jaxpr/ppermute | solution.py:17
  562.5 2.1 select_dynamic-update-slice_fusion.3
  565.6 39.2 %collective-permute-done = bf16[64,2560]{1,0:T(8,128)(2,1)S(1)} collective-permute-done((bf16[64,2560]{1,0:T(8,128)(2,1)}, bf16[64,2560]{1,0:T(8,128)(2,1)S(1)}, u32[]{:S(2)}, u32[]{:S(2)}) %collective-permute-start) | collective-permute-done | bytes 327712 | tf_op jit(solution)/shard_map/while/body/eval_jaxpr/ppermute | solution.py:17
  608.3 51.8 %collective-permute-start.1 = (bf16[64,2560]{1,0:T(8,128)(2,1)}, bf16[64,2560]{1,0:T(8,128)(2,1)}, u32[]{:S(2)}, u32[]{:S(2)}) collective-permute-start(bf16[64,2560]{1,0:T(8,128)(2,1)} %bitcast.557), channel_id=1, source_target_pairs={{0,8},{8,16},{16,24},{24,32},{32,40},{40,48},{48,56},{56,64},{64,7... | collective-permute-start | bytes 983048 | tf_op jit(solution)/shard_map/while/body/eval_jaxpr/ppermute | solution.py:17
  662.9 2.1 select_dynamic-update-slice_fusion.3
  666.1 93.0 %collective-permute-done = bf16[64,2560]{1,0:T(8,128)(2,1)S(1)} collective-permute-done((bf16[64,2560]{1,0:T(8,128)(2,1)}, bf16[64,2560]{1,0:T(8,128)(2,1)S(1)}, u32[]{:S(2)}, u32[]{:S(2)}) %collective-permute-start) | collective-permute-done | bytes 327712 | tf_op jit(solution)/shard_map/while/body/eval_jaxpr/ppermute | solution.py:17
  762.5 51.8 %collective-permute-start.1 = (bf16[64,2560]{1,0:T(8,128)(2,1)}, bf16[64,2560]{1,0:T(8,128)(2,1)}, u32[]{:S(2)}, u32[]{:S(2)}) collective-permute-start(bf16[64,2560]{1,0:T(8,128)(2,1)} %bitcast.557), channel_id=1, source_target_pairs={{0,8},{8,16},{16,24},{24,32},{32,40},{40,48},{48,56},{56,64},{64,7... | collective-permute-start | bytes 983048 | tf_op jit(solution)/shard_map/while/body/eval_jaxpr/ppermute | solution.py:17
  817.1 2.1 select_dynamic-update-slice_fusion.3
  820.3 23.7 %collective-permute-done = bf16[64,2560]{1,0:T(8,128)(2,1)S(1)} collective-permute-done((bf16[64,2560]{1,0:T(8,128)(2,1)}, bf16[64,2560]{1,0:T(8,128)(2,1)S(1)}, u32[]{:S(2)}, u32[]{:S(2)}) %collective-permute-start) | collective-permute-done | bytes 327712 | tf_op jit(solution)/shard_map/while/body/eval_jaxpr/ppermute | solution.py:17
  847.5 41.0 %collective-permute-start.1 = (bf16[64,2560]{1,0:T(8,128)(2,1)}, bf16[64,2560]{1,0:T(8,128)(2,1)}, u32[]{:S(2)}, u32[]{:S(2)}) collective-permute-start(bf16[64,2560]{1,0:T(8,128)(2,1)} %bitcast.557), channel_id=1, source_target_pairs={{0,8},{8,16},{16,24},{24,32},{32,40},{40,48},{48,56},{56,64},{64,7... | collective-permute-start | bytes 983048 | tf_op jit(solution)/shard_map/while/body/eval_jaxpr/ppermute | solution.py:17
  891.2 2.1 select_dynamic-update-slice_fusion.3
  894.4 27.4 %collective-permute-done = bf16[64,2560]{1,0:T(8,128)(2,1)S(1)} collective-permute-done((bf16[64,2560]{1,0:T(8,128)(2,1)}, bf16[64,2560]{1,0:T(8,128)(2,1)S(1)}, u32[]{:S(2)}, u32[]{:S(2)}) %collective-permute-start) | collective-permute-done | bytes 327712 | tf_op jit(solution)/shard_map/while/body/eval_jaxpr/ppermute | solution.py:17
  925.2 8.0 collective-permute-start.1
  933.2 30.7 %conditional.21 = (bf16[1,64,2560]{2,1,0:T(8,128)(2,1)}, f32[2,3,2560]{2,1,0:T(4,128)}) conditional(s32[]{:T(128)} %convert_element_type.1008, () %tuple.187, (s32[]{:T(128)}, bf16[2,1,2,2,64,2560]{5,4,3,2,1,0:T(8,128)(2,1)}, s32[]{:T(128)}, bf16[2,1,2,2,64,2560]{5,4,3,2,1,0:T(8,128)(2,1)}, pred[]{:T(512)}, /*index=5*/s32[2,2,1]{2,1,0:T(2,128)}, ...), branch_computations={%region_5.5_spmd, %region_6.28_spmd} | conditional | flops 245491968 | bytes 122042480 | solution.py:186
  943.1 1.9 fusion.114
  951.8 10.2 conditional.2
  962.3 1.6 add_convert_fusion
  965.3 2.2 select_dynamic-update-slice_fusion.3
  972.0 6.0 collective-permute-start.1
  978.0 30.7 %conditional.21 = (bf16[1,64,2560]{2,1,0:T(8,128)(2,1)}, f32[2,3,2560]{2,1,0:T(4,128)}) conditional(s32[]{:T(128)} %convert_element_type.1008, () %tuple.187, (s32[]{:T(128)}, bf16[2,1,2,2,64,2560]{5,4,3,2,1,0:T(8,128)(2,1)}, s32[]{:T(128)}, bf16[2,1,2,2,64,2560]{5,4,3,2,1,0:T(8,128)(2,1)}, pred[]{:T(512)}, /*index=5*/s32[2,2,1]{2,1,0:T(2,128)}, ...), branch_computations={%region_5.5_spmd, %region_6.28_spmd} | conditional | flops 245491968 | bytes 122042480 | solution.py:186
  987.9 1.9 fusion.114
  996.6 10.2 conditional.2
  1007.1 1.6 add_convert_fusion
  1010.1 2.2 select_dynamic-update-slice_fusion.3
  1017.0 3.9 collective-permute-done.3
  1020.9 5.4 collective-permute-done.4
  1026.3 2.5 maximum_bitcast_fusion.6
  1028.8 2.9 collective-permute-done.5
  1031.7 34.5 %psum.7 = f32[2,3,2560]{2,0,1:T(2,128)S(1)} all-reduce(f32[2,3,2560]{2,0,1:T(2,128)S(1)} %copy_add_fusion), channel_id=1, replica_groups=mesh['section'=16,'dp'=8] {'dp'}, use_global_device_ids=true, to_apply=%region_54.55 | all-reduce | flops 15360 | bytes 122880 | tf_op jit(solution)/shard_map/psum | solution.py:226
  (611 shorter events, 280.8 us)
Async XLA Ops:
  26.0 3.7 copy-start.28
  45.7 8.1 collective-permute-start.1
  49.1 4.7 collective-permute-start
  68.6 3.7 copy-start.28
  88.3 9.8 collective-permute-start.1
  93.4 3.6 copy-start.42
  93.4 3.6 copy-start.44
  93.4 4.7 collective-permute-start
  101.6 43.0 %collective-permute-start.1 = (bf16[64,2560]{1,0:T(8,128)(2,1)}, bf16[64,2560]{1,0:T(8,128)(2,1)}, u32[]{:S(2)}, u32[]{:S(2)}) collective-permute-start(bf16[64,2560]{1,0:T(8,128)(2,1)} %bitcast.557), channel_id=1, source_target_pairs={{0,8},{8,16},{16,24},{24,32},{32,40},{40,48},{48,56},{56,64},{64,7... | collective-permute-start | bytes 983048 | tf_op jit(solution)/shard_map/while/body/eval_jaxpr/ppermute | solution.py:17
  140.0 4.6 collective-permute-start
  148.1 12.0 %collective-permute-start.1 = (bf16[64,2560]{1,0:T(8,128)(2,1)}, bf16[64,2560]{1,0:T(8,128)(2,1)}, u32[]{:S(2)}, u32[]{:S(2)}) collective-permute-start(bf16[64,2560]{1,0:T(8,128)(2,1)} %bitcast.557), channel_id=1, source_target_pairs={{0,8},{8,16},{16,24},{24,32},{32,40},{40,48},{48,56},{56,64},{64,7... | collective-permute-start | bytes 983048 | tf_op jit(solution)/shard_map/while/body/eval_jaxpr/ppermute | solution.py:17
  155.5 33.7 %collective-permute-start = (bf16[64,2560]{1,0:T(8,128)(2,1)}, bf16[64,2560]{1,0:T(8,128)(2,1)S(1)}, u32[]{:S(2)}, u32[]{:S(2)}) collective-permute-start(bf16[64,2560]{1,0:T(8,128)(2,1)} %bitcast.556), channel_id=1, source_target_pairs={{8,0},{16,8},{24,16},{32,24},{40,32},{48,40},{56,48},{64,56},{72,6... | collective-permute-start | bytes 983048 | tf_op jit(solution)/shard_map/while/body/eval_jaxpr/ppermute | solution.py:17
  160.0 29.2 %copy-start.43 = (f32[2,3,2560]{2,1,0:T(4,128)}, f32[2,3,2560]{2,1,0:T(4,128)S(1)}, u32[]{:S(2)}) copy-start(f32[2,3,2560]{2,1,0:T(4,128)S(1)} %get-tuple-element.1680) | copy-start | bytes 184324 | tf_op jit(solution)/shard_map/while
  160.0 29.1 %copy-start.45 = (f32[2,3,2560]{2,1,0:T(4,128)}, f32[2,3,2560]{2,1,0:T(4,128)S(1)}, u32[]{:S(2)}) copy-start(f32[2,3,2560]{2,1,0:T(4,128)S(1)} %get-tuple-element.1679) | copy-start | bytes 184324 | tf_op jit(solution)/shard_map/while
  192.6 14.0 %collective-permute-start.1 = (bf16[64,2560]{1,0:T(8,128)(2,1)}, bf16[64,2560]{1,0:T(8,128)(2,1)}, u32[]{:S(2)}, u32[]{:S(2)}) collective-permute-start(bf16[64,2560]{1,0:T(8,128)(2,1)} %bitcast.557), channel_id=1, source_target_pairs={{0,8},{8,16},{16,24},{24,32},{32,40},{40,48},{48,56},{56,64},{64,7... | collective-permute-start | bytes 983048 | tf_op jit(solution)/shard_map/while/body/eval_jaxpr/ppermute | solution.py:17
  202.0 4.6 collective-permute-start
  210.1 38.5 %collective-permute-start.1 = (bf16[64,2560]{1,0:T(8,128)(2,1)}, bf16[64,2560]{1,0:T(8,128)(2,1)}, u32[]{:S(2)}, u32[]{:S(2)}) collective-permute-start(bf16[64,2560]{1,0:T(8,128)(2,1)} %bitcast.557), channel_id=1, source_target_pairs={{0,8},{8,16},{16,24},{24,32},{32,40},{40,48},{48,56},{56,64},{64,7... | collective-permute-start | bytes 983048 | tf_op jit(solution)/shard_map/while/body/eval_jaxpr/ppermute | solution.py:17
  244.0 21.6 %collective-permute-start = (bf16[64,2560]{1,0:T(8,128)(2,1)}, bf16[64,2560]{1,0:T(8,128)(2,1)S(1)}, u32[]{:S(2)}, u32[]{:S(2)}) collective-permute-start(bf16[64,2560]{1,0:T(8,128)(2,1)} %bitcast.556), channel_id=1, source_target_pairs={{8,0},{16,8},{24,16},{32,24},{40,32},{48,40},{56,48},{64,56},{72,6... | collective-permute-start | bytes 983048 | tf_op jit(solution)/shard_map/while/body/eval_jaxpr/ppermute | solution.py:17
  248.5 17.0 %copy-start.43 = (f32[2,3,2560]{2,1,0:T(4,128)}, f32[2,3,2560]{2,1,0:T(4,128)S(1)}, u32[]{:S(2)}) copy-start(f32[2,3,2560]{2,1,0:T(4,128)S(1)} %get-tuple-element.1680) | copy-start | bytes 184324 | tf_op jit(solution)/shard_map/while
  248.6 17.0 %copy-start.45 = (f32[2,3,2560]{2,1,0:T(4,128)}, f32[2,3,2560]{2,1,0:T(4,128)S(1)}, u32[]{:S(2)}) copy-start(f32[2,3,2560]{2,1,0:T(4,128)S(1)} %get-tuple-element.1679) | copy-start | bytes 184324 | tf_op jit(solution)/shard_map/while
  269.0 17.6 %collective-permute-start.1 = (bf16[64,2560]{1,0:T(8,128)(2,1)}, bf16[64,2560]{1,0:T(8,128)(2,1)}, u32[]{:S(2)}, u32[]{:S(2)}) collective-permute-start(bf16[64,2560]{1,0:T(8,128)(2,1)} %bitcast.557), channel_id=1, source_target_pairs={{0,8},{8,16},{16,24},{24,32},{32,40},{40,48},{48,56},{56,64},{64,7... | collective-permute-start | bytes 983048 | tf_op jit(solution)/shard_map/while/body/eval_jaxpr/ppermute | solution.py:17
  282.0 52.8 %collective-permute-start = (bf16[64,2560]{1,0:T(8,128)(2,1)}, bf16[64,2560]{1,0:T(8,128)(2,1)S(1)}, u32[]{:S(2)}, u32[]{:S(2)}) collective-permute-start(bf16[64,2560]{1,0:T(8,128)(2,1)} %bitcast.556), channel_id=1, source_target_pairs={{8,0},{16,8},{24,16},{32,24},{40,32},{48,40},{56,48},{64,56},{72,6... | collective-permute-start | bytes 983048 | tf_op jit(solution)/shard_map/while/body/eval_jaxpr/ppermute | solution.py:17
  286.6 48.2 %copy-start.43 = (f32[2,3,2560]{2,1,0:T(4,128)}, f32[2,3,2560]{2,1,0:T(4,128)S(1)}, u32[]{:S(2)}) copy-start(f32[2,3,2560]{2,1,0:T(4,128)S(1)} %get-tuple-element.1680) | copy-start | bytes 184324 | tf_op jit(solution)/shard_map/while
  286.6 48.2 %copy-start.45 = (f32[2,3,2560]{2,1,0:T(4,128)}, f32[2,3,2560]{2,1,0:T(4,128)S(1)}, u32[]{:S(2)}) copy-start(f32[2,3,2560]{2,1,0:T(4,128)S(1)} %get-tuple-element.1679) | copy-start | bytes 184324 | tf_op jit(solution)/shard_map/while
  338.2 17.6 %collective-permute-start.1 = (bf16[64,2560]{1,0:T(8,128)(2,1)}, bf16[64,2560]{1,0:T(8,128)(2,1)}, u32[]{:S(2)}, u32[]{:S(2)}) collective-permute-start(bf16[64,2560]{1,0:T(8,128)(2,1)} %bitcast.557), channel_id=1, source_target_pairs={{0,8},{8,16},{16,24},{24,32},{32,40},{40,48},{48,56},{56,64},{64,7... | collective-permute-start | bytes 983048 | tf_op jit(solution)/shard_map/while/body/eval_jaxpr/ppermute | solution.py:17
  351.3 4.6 collective-permute-start
  359.3 38.5 %collective-permute-start.1 = (bf16[64,2560]{1,0:T(8,128)(2,1)}, bf16[64,2560]{1,0:T(8,128)(2,1)}, u32[]{:S(2)}, u32[]{:S(2)}) collective-permute-start(bf16[64,2560]{1,0:T(8,128)(2,1)} %bitcast.557), channel_id=1, source_target_pairs={{0,8},{8,16},{16,24},{24,32},{32,40},{40,48},{48,56},{56,64},{64,7... | collective-permute-start | bytes 983048 | tf_op jit(solution)/shard_map/while/body/eval_jaxpr/ppermute | solution.py:17
  393.3 4.6 collective-permute-start
  401.3 12.0 %collective-permute-start.1 = (bf16[64,2560]{1,0:T(8,128)(2,1)}, bf16[64,2560]{1,0:T(8,128)(2,1)}, u32[]{:S(2)}, u32[]{:S(2)}) collective-permute-start(bf16[64,2560]{1,0:T(8,128)(2,1)} %bitcast.557), channel_id=1, source_target_pairs={{0,8},{8,16},{16,24},{24,32},{32,40},{40,48},{48,56},{56,64},{64,7... | collective-permute-start | bytes 983048 | tf_op jit(solution)/shard_map/while/body/eval_jaxpr/ppermute | solution.py:17
  408.7 49.1 %collective-permute-start = (bf16[64,2560]{1,0:T(8,128)(2,1)}, bf16[64,2560]{1,0:T(8,128)(2,1)S(1)}, u32[]{:S(2)}, u32[]{:S(2)}) collective-permute-start(bf16[64,2560]{1,0:T(8,128)(2,1)} %bitcast.556), channel_id=1, source_target_pairs={{8,0},{16,8},{24,16},{32,24},{40,32},{48,40},{56,48},{64,56},{72,6... | collective-permute-start | bytes 983048 | tf_op jit(solution)/shard_map/while/body/eval_jaxpr/ppermute | solution.py:17
  413.3 44.6 %copy-start.43 = (f32[2,3,2560]{2,1,0:T(4,128)}, f32[2,3,2560]{2,1,0:T(4,128)S(1)}, u32[]{:S(2)}) copy-start(f32[2,3,2560]{2,1,0:T(4,128)S(1)} %get-tuple-element.1680) | copy-start | bytes 184324 | tf_op jit(solution)/shard_map/while
  413.3 44.6 %copy-start.45 = (f32[2,3,2560]{2,1,0:T(4,128)}, f32[2,3,2560]{2,1,0:T(4,128)S(1)}, u32[]{:S(2)}) copy-start(f32[2,3,2560]{2,1,0:T(4,128)S(1)} %get-tuple-element.1679) | copy-start | bytes 184324 | tf_op jit(solution)/shard_map/while
  461.3 21.7 %collective-permute-start.1 = (bf16[64,2560]{1,0:T(8,128)(2,1)}, bf16[64,2560]{1,0:T(8,128)(2,1)}, u32[]{:S(2)}, u32[]{:S(2)}) collective-permute-start(bf16[64,2560]{1,0:T(8,128)(2,1)} %bitcast.557), channel_id=1, source_target_pairs={{0,8},{8,16},{16,24},{24,32},{32,40},{40,48},{48,56},{56,64},{64,7... | collective-permute-start | bytes 983048 | tf_op jit(solution)/shard_map/while/body/eval_jaxpr/ppermute | solution.py:17
  478.4 4.6 collective-permute-start
  486.4 79.2 %collective-permute-start.1 = (bf16[64,2560]{1,0:T(8,128)(2,1)}, bf16[64,2560]{1,0:T(8,128)(2,1)}, u32[]{:S(2)}, u32[]{:S(2)}) collective-permute-start(bf16[64,2560]{1,0:T(8,128)(2,1)} %bitcast.557), channel_id=1, source_target_pairs={{0,8},{8,16},{16,24},{24,32},{32,40},{40,48},{48,56},{56,64},{64,7... | collective-permute-start | bytes 983048 | tf_op jit(solution)/shard_map/while/body/eval_jaxpr/ppermute | solution.py:17
  561.0 43.8 %collective-permute-start = (bf16[64,2560]{1,0:T(8,128)(2,1)}, bf16[64,2560]{1,0:T(8,128)(2,1)S(1)}, u32[]{:S(2)}, u32[]{:S(2)}) collective-permute-start(bf16[64,2560]{1,0:T(8,128)(2,1)} %bitcast.556), channel_id=1, source_target_pairs={{8,0},{16,8},{24,16},{32,24},{40,32},{48,40},{56,48},{64,56},{72,6... | collective-permute-start | bytes 983048 | tf_op jit(solution)/shard_map/while/body/eval_jaxpr/ppermute | solution.py:17
  565.6 39.3 %copy-start.43 = (f32[2,3,2560]{2,1,0:T(4,128)}, f32[2,3,2560]{2,1,0:T(4,128)S(1)}, u32[]{:S(2)}) copy-start(f32[2,3,2560]{2,1,0:T(4,128)S(1)} %get-tuple-element.1680) | copy-start | bytes 184324 | tf_op jit(solution)/shard_map/while
  565.6 39.3 %copy-start.45 = (f32[2,3,2560]{2,1,0:T(4,128)}, f32[2,3,2560]{2,1,0:T(4,128)S(1)}, u32[]{:S(2)}) copy-start(f32[2,3,2560]{2,1,0:T(4,128)S(1)} %get-tuple-element.1679) | copy-start | bytes 184324 | tf_op jit(solution)/shard_map/while
  608.3 57.8 %collective-permute-start.1 = (bf16[64,2560]{1,0:T(8,128)(2,1)}, bf16[64,2560]{1,0:T(8,128)(2,1)}, u32[]{:S(2)}, u32[]{:S(2)}) collective-permute-start(bf16[64,2560]{1,0:T(8,128)(2,1)} %bitcast.557), channel_id=1, source_target_pairs={{0,8},{8,16},{16,24},{24,32},{32,40},{40,48},{48,56},{56,64},{64,7... | collective-permute-start | bytes 983048 | tf_op jit(solution)/shard_map/while/body/eval_jaxpr/ppermute | solution.py:17
  661.5 97.6 %collective-permute-start = (bf16[64,2560]{1,0:T(8,128)(2,1)}, bf16[64,2560]{1,0:T(8,128)(2,1)S(1)}, u32[]{:S(2)}, u32[]{:S(2)}) collective-permute-start(bf16[64,2560]{1,0:T(8,128)(2,1)} %bitcast.556), channel_id=1, source_target_pairs={{8,0},{16,8},{24,16},{32,24},{40,32},{48,40},{56,48},{64,56},{72,6... | collective-permute-start | bytes 983048 | tf_op jit(solution)/shard_map/while/body/eval_jaxpr/ppermute | solution.py:17
  666.0 93.0 %copy-start.43 = (f32[2,3,2560]{2,1,0:T(4,128)}, f32[2,3,2560]{2,1,0:T(4,128)S(1)}, u32[]{:S(2)}) copy-start(f32[2,3,2560]{2,1,0:T(4,128)S(1)} %get-tuple-element.1680) | copy-start | bytes 184324 | tf_op jit(solution)/shard_map/while
  666.0 93.0 %copy-start.45 = (f32[2,3,2560]{2,1,0:T(4,128)}, f32[2,3,2560]{2,1,0:T(4,128)S(1)}, u32[]{:S(2)}) copy-start(f32[2,3,2560]{2,1,0:T(4,128)S(1)} %get-tuple-element.1679) | copy-start | bytes 184324 | tf_op jit(solution)/shard_map/while
  762.5 57.8 %collective-permute-start.1 = (bf16[64,2560]{1,0:T(8,128)(2,1)}, bf16[64,2560]{1,0:T(8,128)(2,1)}, u32[]{:S(2)}, u32[]{:S(2)}) collective-permute-start(bf16[64,2560]{1,0:T(8,128)(2,1)} %bitcast.557), channel_id=1, source_target_pairs={{0,8},{8,16},{16,24},{24,32},{32,40},{40,48},{48,56},{56,64},{64,7... | collective-permute-start | bytes 983048 | tf_op jit(solution)/shard_map/while/body/eval_jaxpr/ppermute | solution.py:17
  815.7 28.3 %collective-permute-start = (bf16[64,2560]{1,0:T(8,128)(2,1)}, bf16[64,2560]{1,0:T(8,128)(2,1)S(1)}, u32[]{:S(2)}, u32[]{:S(2)}) collective-permute-start(bf16[64,2560]{1,0:T(8,128)(2,1)} %bitcast.556), channel_id=1, source_target_pairs={{8,0},{16,8},{24,16},{32,24},{40,32},{48,40},{56,48},{64,56},{72,6... | collective-permute-start | bytes 983048 | tf_op jit(solution)/shard_map/while/body/eval_jaxpr/ppermute | solution.py:17
  820.3 23.8 %copy-start.43 = (f32[2,3,2560]{2,1,0:T(4,128)}, f32[2,3,2560]{2,1,0:T(4,128)S(1)}, u32[]{:S(2)}) copy-start(f32[2,3,2560]{2,1,0:T(4,128)S(1)} %get-tuple-element.1680) | copy-start | bytes 184324 | tf_op jit(solution)/shard_map/while
  820.3 23.8 %copy-start.45 = (f32[2,3,2560]{2,1,0:T(4,128)}, f32[2,3,2560]{2,1,0:T(4,128)S(1)}, u32[]{:S(2)}) copy-start(f32[2,3,2560]{2,1,0:T(4,128)S(1)} %get-tuple-element.1679) | copy-start | bytes 184324 | tf_op jit(solution)/shard_map/while
  847.5 46.9 %collective-permute-start.1 = (bf16[64,2560]{1,0:T(8,128)(2,1)}, bf16[64,2560]{1,0:T(8,128)(2,1)}, u32[]{:S(2)}, u32[]{:S(2)}) collective-permute-start(bf16[64,2560]{1,0:T(8,128)(2,1)} %bitcast.557), channel_id=1, source_target_pairs={{0,8},{8,16},{16,24},{24,32},{32,40},{40,48},{48,56},{56,64},{64,7... | collective-permute-start | bytes 983048 | tf_op jit(solution)/shard_map/while/body/eval_jaxpr/ppermute | solution.py:17
  889.8 31.9 %collective-permute-start = (bf16[64,2560]{1,0:T(8,128)(2,1)}, bf16[64,2560]{1,0:T(8,128)(2,1)S(1)}, u32[]{:S(2)}, u32[]{:S(2)}) collective-permute-start(bf16[64,2560]{1,0:T(8,128)(2,1)} %bitcast.556), channel_id=1, source_target_pairs={{8,0},{16,8},{24,16},{32,24},{40,32},{48,40},{56,48},{64,56},{72,6... | collective-permute-start | bytes 983048 | tf_op jit(solution)/shard_map/while/body/eval_jaxpr/ppermute | solution.py:17
  894.3 27.4 %copy-start.43 = (f32[2,3,2560]{2,1,0:T(4,128)}, f32[2,3,2560]{2,1,0:T(4,128)S(1)}, u32[]{:S(2)}) copy-start(f32[2,3,2560]{2,1,0:T(4,128)S(1)} %get-tuple-element.1680) | copy-start | bytes 184324 | tf_op jit(solution)/shard_map/while
  894.4 27.4 %copy-start.45 = (f32[2,3,2560]{2,1,0:T(4,128)}, f32[2,3,2560]{2,1,0:T(4,128)S(1)}, u32[]{:S(2)}) copy-start(f32[2,3,2560]{2,1,0:T(4,128)S(1)} %get-tuple-element.1679) | copy-start | bytes 184324 | tf_op jit(solution)/shard_map/while
  925.2 43.4 %collective-permute-start.1 = (bf16[64,2560]{1,0:T(8,128)(2,1)}, bf16[64,2560]{1,0:T(8,128)(2,1)}, u32[]{:S(2)}, u32[]{:S(2)}) collective-permute-start(bf16[64,2560]{1,0:T(8,128)(2,1)} %bitcast.557), channel_id=1, source_target_pairs={{0,8},{8,16},{16,24},{24,32},{32,40},{40,48},{48,56},{56,64},{64,7... | collective-permute-start | bytes 983048 | tf_op jit(solution)/shard_map/while/body/eval_jaxpr/ppermute | solution.py:17
  945.0 3.7 copy-start.29
  963.9 3.6 copy-start.44
  963.9 4.7 collective-permute-start
  972.0 41.3 %collective-permute-start.1 = (bf16[64,2560]{1,0:T(8,128)(2,1)}, bf16[64,2560]{1,0:T(8,128)(2,1)}, u32[]{:S(2)}, u32[]{:S(2)}) collective-permute-start(bf16[64,2560]{1,0:T(8,128)(2,1)} %bitcast.557), channel_id=1, source_target_pairs={{0,8},{8,16},{16,24},{24,32},{32,40},{40,48},{48,56},{56,64},{64,7... | collective-permute-start | bytes 983048 | tf_op jit(solution)/shard_map/while/body/eval_jaxpr/ppermute | solution.py:17
  989.8 3.7 copy-start.29
  1008.6 3.6 copy-start.42
  1008.6 3.6 copy-start.44
  1008.7 4.7 collective-permute-start
  1015.0 2.0 collective-permute-start.2
  1017.0 3.9 collective-permute-start.3
  1020.9 5.4 collective-permute-start.4
  1026.3 5.4 collective-permute-start.5
  1026.3 5.4 copy-start.46
  (98 other events, 185.5 us)
where the time goes:
time: 1070 us
  starting transfers between devices  424 us (40%)
  waiting for transfers between devices  335 us (31%)
  local copies, waits for them, and re-layouts  147 us (14%)
  other arithmetic  104 us (10%)
  blocking collectives  34.5 us (3%)
  matrix products  14.1 us (1%)
    ppermute x34, starting transfers between devices, from_behind(): lax.ppermute(value, axis, [(source, source + steps) for source in range(i...  423 us
    ppermute x34, waiting for transfers between devices, from_behind(): lax.ppermute(value, axis, [(source, source + steps) for source in range(i...  322 us
    another operation x104, local copies, waits for them, and re-layouts  55.9 us
    dynamic_update_slice x17, other arithmetic, run_direction(): written = lax.dynamic_update_index_in_dim(written, kept_grad, chosen, 0)  35.9 us
    psum x1, blocking collectives, body(): own_rows = lax.psum(own_terms + mirrored, 'dp')  34.5 us
  transfers between devices with their start and end apart: 38, of which 12 were waited for; matrix products, arithmetic and copies ran while one was open for 12% of the time, Pallas kernels for 0%

commit v1 on v0

v1 whole, which is shorter than its diff:
```python
import functools
import math

import jax
import jax.numpy as jnp
from jax import lax
from jax.experimental import pallas as pl
from jax.experimental.pallas import tpu as pltpu
from jax.sharding import PartitionSpec as P

HEAD_DIM = 128
PAIR = 2 * HEAD_DIM
EPSILON = 1e-06
MESH = pl.DeviceIdType.MESH
F32 = jnp.float32
BF16 = jnp.bfloat16


def blocks_apart(pair):
    zero = jnp.zeros((pair.shape[0], HEAD_DIM), pair.dtype)
    upper = jnp.concatenate([pair[:, :HEAD_DIM], zero], axis=1)
    lower = jnp.concatenate([zero, pair[:, HEAD_DIM:]], axis=1)
    return jnp.concatenate([upper, lower], axis=0)


def dot(left, right, left_dim, right_dim):
    return lax.dot_general(
        left, right, (((left_dim,), (right_dim,)), ((), ())), preferred_element_type=F32
    )


def kernel(
    sections,
    layers_ref,
    lengths_ref,
    gains_ref,
    queries_hbm,
    keys_hbm,
    inputs_hbm,
    cotangents_hbm,
    grads_hbm,
    terms_ref,
    q_buf,
    k_buf,
    h_buf,
    v_buf,
    p_wide,
    p_low,
    r_buf,
    e_buf,
    x_buf,
    g_buf,
    load_sems,
    seed_sems,
    op_send,
    op_recv,
    hop_send,
    hop_recv,
    set_send,
    set_recv,
    out_sems,
):
    place = lax.axis_index("section")
    core = lax.rem(place, 2)
    chip = lax.div(place, 2)
    chips = sections // 2
    seq = q_buf.shape[3]
    width = q_buf.shape[4]
    pairs = width // PAIR
    layer_total = layers_ref.shape[0]
    scale = 1.0 / math.sqrt(HEAD_DIM)
    partner = {"section": place + 1 - 2 * core}
    first_direction = jnp.where(chip >= chips // 2, 0, 1)
    leads = (chip == chips - 1) | (chip == 0)

    barrier = pltpu.get_barrier_semaphore()
    pl.semaphore_signal(barrier, inc=1, device_id=partner, device_id_type=MESH)

    @pl.when(chip > 0)
    def _():
        pl.semaphore_signal(barrier, inc=1, device_id={"section": place - 2}, device_id_type=MESH)

    @pl.when(chip < chips - 1)
    def _():
        pl.semaphore_signal(barrier, inc=1, device_id={"section": place + 2}, device_id_type=MESH)

    def loads(d, m):
        copies = [pltpu.make_async_copy(inputs_hbm.at[d, 0, m], h_buf.at[d, m, 0], load_sems.at[d, m, 0])]
        for slot in range(2):
            copies.append(
                pltpu.make_async_copy(
                    keys_hbm.at[d, 0, slot, m], k_buf.at[d, m, slot], load_sems.at[d, m, 1 + 2 * slot]
                )
            )
            copies.append(
                pltpu.make_async_copy(
                    queries_hbm.at[d, 0, slot, m], q_buf.at[d, m, slot], load_sems.at[d, m, 2 + 2 * slot]
                )
            )
        return copies

    def seed(d):
        return pltpu.make_async_copy(cotangents_hbm.at[d, core], e_buf.at[d, 0], seed_sems.at[d])

    for phase in range(2):
        d = first_direction if phase == 0 else 1 - first_direction
        for m in (1 - core, core):
            for copy in loads(d, m):
                copy.start()
        if phase == 0:

            @pl.when(leads)
            def _():
                seed(d).start()

    for d in range(2):
        for whose in range(2):
            at = place if whose == 0 else place + 1 - 2 * core
            block = at if d == 0 else sections - 1 - at
            before = jnp.int32(0)
            for layer in range(layer_total):
                before = before + jnp.where(layers_ref[layer] < block, 1, 0)
            for slot in range(2):
                layer = jnp.minimum(before + slot, layer_total - 1)
                g_buf[d, whose, slot, 0:3, :] = gains_ref[layer]

    terms_ref[...] = jnp.zeros_like(terms_ref)

    def second_layer(d):
        block = jnp.where(d == 0, place, sections - 1 - place)
        count = jnp.int32(0)
        for layer in range(layer_total):
            count = count + jnp.where(layers_ref[layer] == block, 1, 0)
        return count == 2

    neighbours = 1 + jnp.where(chip > 0, 1, 0) + jnp.where(chip < chips - 1, 1, 0)
    pl.semaphore_wait(barrier, neighbours)

    def operand_copies(d):
        mine = 1 - core
        parts = (
            (p_low.at[d, mine], p_low.at[d, 2]),
            (h_buf.at[d, mine, 0:2], h_buf.at[d, 2, 0:2]),
            (r_buf.at[d, mine], r_buf.at[d, 2]),
        )
        return [
            pltpu.make_async_remote_copy(
                src_ref=source,
                dst_ref=target,
                send_sem=op_send.at[d, at],
                recv_sem=op_recv.at[d, at],
                device_id=partner,
                device_id_type=MESH,
            )
            for at, (source, target) in enumerate(parts)
        ]

    def hop(d):
        step = jnp.where(d == 0, -2, 2)
        return pltpu.make_async_remote_copy(
            src_ref=e_buf.at[d, 4],
            dst_ref=e_buf.at[d, 0],
            send_sem=hop_send.at[d],
            recv_sem=hop_recv.at[d],
            device_id={"section": place + step},
            device_id_type=MESH,
        )

    def own_base(d):
        return jnp.where(core == 1 - d, 0, 2)

    def set_copy(d):
        return pltpu.make_async_remote_copy(
            src_ref=e_buf.at[d, pl.ds(2 - own_base(d), 3)],
            dst_ref=e_buf.at[d, 5:8],
            send_sem=set_send.at[d],
            recv_sem=set_recv.at[d],
            device_id=partner,
            device_id_type=MESH,
        )

    def out_copies(d):
        return (
            pltpu.make_async_copy(
                e_buf.at[d, own_base(d) + 2], grads_hbm.at[d, 0, core], out_sems.at[d, 0]
            ),
            pltpu.make_async_copy(e_buf.at[d, 7], grads_hbm.at[d, 0, 1 - core], out_sems.at[d, 1]),
        )

    def lane_spread(column):
        return jnp.broadcast_to(column, (seq, HEAD_DIM))

    def prepare(d):
        two = second_layer(d)

        @pl.loop(0, 2)
        def _(turn):
            m = jnp.where(turn == 0, 1 - core, core)
            for copy in loads(d, m):
                copy.wait()
            length = lengths_ref[d, m, 0]
            key_at = lax.broadcasted_iota(jnp.int32, (seq, 2 * seq), 0)
            query_at = lax.rem(lax.broadcasted_iota(jnp.int32, (seq, 2 * seq), 1), seq)
            allowed = (key_at <= query_at) & (key_at < length)

            @pl.loop(0, 2)
            def _(slot):
                squares = jnp.zeros((seq, HEAD_DIM), F32)
                for tile in range(width // HEAD_DIM):
                    part = h_buf[d, m, slot, :, tile * HEAD_DIM : (tile + 1) * HEAD_DIM].astype(F32)
                    squares = squares + part * part
                inverse = lax.rsqrt(jnp.sum(squares, axis=1, keepdims=True) * (1.0 / width) + EPSILON)
                spread = lane_spread(inverse)
                spread_two = jnp.concatenate([spread, spread], axis=1)
                present = (slot == 0) | two
                r_buf[d, m, slot] = jnp.where(present, spread, 0.0)
                for pair in range(pairs):
                    cols = slice(pair * PAIR, (pair + 1) * PAIR)
                    state = h_buf[d, m, slot, :, cols].astype(F32)
                    values = (state * spread_two * g_buf[d, 0, slot, 0:1, cols]).astype(BF16)
                    v_buf[d, m, slot, :, cols] = values
                    scaled_q = (q_buf[d, m, slot, :, cols].astype(F32) * g_buf[d, 0, slot, 1:2, cols]).astype(BF16)
                    scaled_k = (k_buf[d, m, slot, :, cols].astype(F32) * g_buf[d, 0, slot, 2:3, cols]).astype(BF16)
                    scores = dot(scaled_k, blocks_apart(scaled_q), 1, 1) * scale
                    masked = jnp.where(allowed, scores, -1e30)
                    top = jnp.max(masked, axis=0, keepdims=True)
                    terms = jnp.where(allowed, jnp.exp(masked - top), 0.0)
                    probs = terms * (1.0 / jnp.sum(terms, axis=0, keepdims=True))
                    low = probs.astype(BF16)
                    p_wide[d, m, slot, pair] = probs
                    p_low[d, m, slot, pair] = low
                    mixed = dot(low, values, 0, 0)
                    mixed = jnp.concatenate([mixed[:seq, :HEAD_DIM], mixed[seq:, HEAD_DIM:]], axis=1)
                    h_buf[d, m, slot + 1, :, cols] = (state + mixed).astype(BF16)

            @pl.when(turn == 0)
            def _():
                for copy in operand_copies(d):
                    copy.start()

    def chain(d):
        leading = jnp.where(d == 0, chip == chips - 1, chip == 0)

        @pl.when(leading)
        def _():
            seed(d).wait()
            length = lengths_ref[d, core, 0]
            rows = lax.broadcasted_iota(jnp.int32, (seq, PAIR), 0)
            for pair in range(pairs):
                cols = slice(pair * PAIR, (pair + 1) * PAIR)
                drawn = e_buf[d, 0, :, cols].astype(F32)
                e_buf[d, 0, :, cols] = jnp.where(rows < length, drawn, 0.0).astype(BF16)

        for copy in operand_copies(d):
            copy.wait_recv()

        @pl.when(jnp.logical_not(leading))
        def _():
            hop(d).wait_recv()

        @pl.loop(0, 4)
        def _(step):
            visited = lax.rem(lax.div(step, 2) + 1 - d, 2)
            slot = 1 - lax.rem(step, 2)
            entry = jnp.where(visited == core, core, 2)
            whose = jnp.where(visited == core, 0, 1)
            total = jnp.zeros((seq, HEAD_DIM), F32)
            for pair in range(pairs):
                cols = slice(pair * PAIR, (pair + 1) * PAIR)
                grad = e_buf[d, step, :, cols]
                product = dot(p_low[d, entry, slot, pair], blocks_apart(grad), 1, 0)
                product = product * g_buf[d, whose, slot, 0:1, cols]
                x_buf[:, cols] = product
                weighed = product * h_buf[d, entry, slot, :, cols].astype(F32)
                total = total + (weighed[:, :HEAD_DIM] + weighed[:, HEAD_DIM:])
            inverse = r_buf[d, entry, slot]
            shift = lane_spread(jnp.sum(total, axis=1, keepdims=True) * (1.0 / width))
            shift = shift * inverse * inverse * inverse
            for tile in range(width // HEAD_DIM):
                cols = slice(tile * HEAD_DIM, (tile + 1) * HEAD_DIM)
                state = h_buf[d, entry, slot, :, cols].astype(F32)
                grad = e_buf[d, step, :, cols].astype(F32)
                e_buf[d, step + 1, :, cols] = (grad + (inverse * x_buf[:, cols] - state * shift)).astype(BF16)

        ending = jnp.where(d == 0, chip == 0, chip == chips - 1)

        @pl.when(jnp.logical_not(ending))
        def _():
            hop(d).start()

        set_copy(d).start()
        out_copies(d)[0].start()

    def gain_terms(d):
        two = second_layer(d)

        @pl.loop(0, 2)
        def _(turn):
            m = jnp.where(turn == 0, core, 1 - core)
            base = jnp.where(turn == 0, own_base(d), 5)

            @pl.when(turn == 1)
            def _():
                set_copy(d).wait_recv()
                out_copies(d)[1].start()

            @pl.loop(0, 2)
            def _(slot):
                at = base + 1 - slot
                inverse = r_buf[d, m, slot]
                inverse_two = jnp.concatenate([inverse, inverse], axis=1)
                for pair in range(pairs):
                    cols = slice(pair * PAIR, (pair + 1) * PAIR)
                    grad = blocks_apart(e_buf[d, at, :, cols])
                    value_grad = dot(p_low[d, m, slot, pair], grad, 1, 0)
                    normed = h_buf[d, m, slot, :, cols].astype(F32) * inverse_two
                    norm_term = jnp.sum(value_grad * normed, axis=0, keepdims=True)
                    probs_grad = dot(v_buf[d, m, slot, :, cols], grad, 1, 1)
                    probs = p_wide[d, m, slot, pair]
                    delta = jnp.sum(probs * probs_grad, axis=0, keepdims=True)
                    score_grad = (probs * (probs_grad - delta) * scale).astype(BF16)
                    met = dot(score_grad, blocks_apart(q_buf[d, m, slot, :, cols]), 1, 0)
                    shared = jnp.sum(met * k_buf[d, m, slot, :, cols].astype(F32), axis=0, keepdims=True)
                    shared = jnp.where((slot == 0) | two, shared, 0.0)
                    terms_ref[d, slot, 0:1, cols] += norm_term
                    terms_ref[d, slot, 1:2, cols] += shared * g_buf[d, 0, slot, 2:3, cols]
                    terms_ref[d, slot, 2:3, cols] += shared * g_buf[d, 0, slot, 1:2, cols]

    early = leads & (core == 0)

    @pl.loop(0, 6)
    def _(t):
        chain_first = jnp.where(early, 1, 2)
        is_chain = (t == chain_first) | (t == 4)
        is_terms = (t == 3) | (t == 5)
        late = (t >= 4) | ((t >= 1) & (t <= 2) & (t != chain_first))
        d = jnp.where(late, 1 - first_direction, first_direction)

        @pl.when(is_chain)
        def _():
            chain(d)

        @pl.when(is_terms)
        def _():
            gain_terms(d)

        @pl.when(jnp.logical_not(is_chain | is_terms))
        def _():
            prepare(d)

    for d in range(2):
        for copy in operand_copies(d):
            copy.wait_send()
        set_copy(d).wait_send()
        for copy in out_copies(d):
            copy.wait()
        ending = (chip == 0) if d == 0 else (chip == chips - 1)

        @pl.when(jnp.logical_not(ending))
        def _():
            hop(d).wait_send()


def body(
    section_of_layer, lengths, layer_gains, saved_queries, saved_keys, block_inputs, cotangents
):
    sections = lax.axis_size("section")
    groups = lax.axis_size("dp")
    seq, width = block_inputs.shape[3:]
    pairs = width // PAIR
    anywhere = pl.BlockSpec(memory_space=pl.ANY)
    scalars = pl.BlockSpec(memory_space=pltpu.SMEM)
    vector = pl.BlockSpec(memory_space=pltpu.VMEM)
    dma = pltpu.SemaphoreType.DMA
    input_grads, terms = pl.pallas_call(
        functools.partial(kernel, sections),
        out_shape=(
            jax.ShapeDtypeStruct(block_inputs.shape, BF16),
            jax.ShapeDtypeStruct((2, 2, 8, width), F32),
        ),
        in_specs=[scalars, scalars, vector, anywhere, anywhere, anywhere, anywhere],
        out_specs=(anywhere, vector),
        scratch_shapes=[
            pltpu.VMEM((2, 2, 2, seq, width), BF16),
            pltpu.VMEM((2, 2, 2, seq, width), BF16),
            pltpu.VMEM((2, 3, 3, seq, width), BF16),
            pltpu.VMEM((2, 2, 2, seq, width), BF16),
            pltpu.VMEM((2, 2, 2, pairs, seq, 2 * seq), F32),
            pltpu.VMEM((2, 3, 2, pairs, seq, 2 * seq), BF16),
            pltpu.VMEM((2, 3, 2, seq, HEAD_DIM), F32),
            pltpu.VMEM((2, 8, seq, width), BF16),
            pltpu.VMEM((seq, width), F32),
            pltpu.VMEM((2, 2, 2, 8, width), F32),
            dma((2, 2, 5)),
            dma((2,)),
            dma((2, 3)),
            dma((2, 3)),
            dma((2,)),
            dma((2,)),
            dma((2,)),
            dma((2,)),
            dma((2, 2)),
        ],
        compiler_params=pltpu.CompilerParams(
            collective_id=0, has_side_effects=True, vmem_limit_bytes=60000 * 1024
        ),
    )(section_of_layer, lengths, layer_gains, saved_queries, saved_keys, block_inputs, cotangents)
    mirrored = lax.ppermute(
        terms[1], "section", [(at, sections - 1 - at) for at in range(sections)]
    )
    own_rows = lax.psum(terms[0] + mirrored, "dp")
    gain_grads = (own_rows[:, 0:3] / groups)[None]
    return (input_grads, gain_grads)


def solution(mesh):
    in_specs = (
        P(),
        P(None, None, "dp"),
        P(),
        P(None, "section", None, None, "dp", None),
        P(None, "section", None, None, "dp", None),
        P(None, "section", None, "dp", None),
        P(None, None, "dp", None),
    )
    out_specs = (P(None, "section", None, "dp", None), P("section", None, None, None))
    return jax.shard_map(body, mesh=mesh, in_specs=in_specs, out_specs=out_specs, check_vma=False)
```

time: 1070 us -> 190 us (0.18)
  starting transfers between devices: 424 us -> 0.8 us
  waiting for transfers between devices: 335 us -> 78.6 us
  local copies, waits for them, and re-layouts: 147 us -> 7.14 us
  other arithmetic: 104 us -> 2.54 us
  Pallas kernels: 0 us -> 86.6 us
  blocking collectives: 34.5 us -> 0 us
  matrix products: 14.1 us -> 0 us
  between operations: 3.29 us -> 14.1 us
    ppermute x38 -> x1, starting transfers between devices: 424 us -> 0.76 us  [body(): lax.ppermute(terms[1], 'section', [(at, sections - 1 - at) for at in rang...]
    ppermute x38 -> x1, waiting for transfers between devices: 335 us -> 8.07 us  [body(): lax.ppermute(terms[1], 'section', [(at, sections - 1 - at) for at in rang...]
    pallas_call x0 -> x1, Pallas kernels: none -> 86.6 us  [body(): pl.pallas_call(functools.partial(kernel, sections), out_shape=(jax.ShapeD...]
    psum x0 -> x1, waiting for transfers between devices: none -> 70.5 us  [body(): own_rows = lax.psum(terms[0] + mirrored, 'dp')]
    another operation x112 -> x0, local copies, waits for them, and re-layouts: 58.5 us -> none
    dynamic_update_slice x17 -> x0, other arithmetic: 35.9 us -> none  [run_direction(): written = lax.dynamic_update_index_in_dim(written, kept_grad, chosen, 0)]
    psum x1 -> x0, blocking collectives: 34.5 us -> none  [body(): own_rows = lax.psum(own_terms + mirrored, 'dp')]
    convert_element_type x28 -> x0, other arithmetic: 29.9 us -> none  [the longest x8 10.9 us: layer_parts(): (query_in.astype(jnp.float32) * gain_rows[1]).astype(jnp.bfloat16)]
  transfers between devices with their start and end apart: 38 -> 2, of which waited for: 12 -> 2; matrix products, arithmetic and copies ran while one was open for 12% -> 0% of each run, Pallas kernels for 0% -> 0%
where the time goes in v1:
time: 190 us
  Pallas kernels  86.6 us (46%)
  waiting for transfers between devices  78.6 us (41%)
  between operations  14.1 us (7%)
  local copies, waits for them, and re-layouts  7.14 us (4%)
  other arithmetic  2.54 us (1%)
    pallas_call x1, Pallas kernels, body(): pl.pallas_call(functools.partial(kernel, sections), out_shape=(jax.ShapeD...  86.6 us
    psum x1, waiting for transfers between devices, body(): own_rows = lax.psum(terms[0] + mirrored, 'dp')  70.5 us
    ppermute x1, waiting for transfers between devices, body(): lax.ppermute(terms[1], 'section', [(at, sections - 1 - at) for at in rang...  8.07 us
    unnamed x6, local copies, waits for them, and re-layouts  6.22 us
  transfers between devices with their start and end apart: 2, of which 2 were waited for; matrix products, arithmetic and copies ran while one was open for 0% of the time, Pallas kernels for 0%

profile of v1, /device:TPU:0, one launch (start us, length us, event | category | flops | bytes accessed | tf_op | source)
XLA Modules:
  0.0 189.8 jit_solution(16784366128887818398)
XLA Ops:
  7.2 0.0 copy-start
  7.2 0.0 all-reduce.2.cloned.1.call-start
  7.2 2.4 %copy.10.gains_ref = f32[20,3,2560]{2,1,0:T(4,128)} copy(f32[20,3,2560]{2,0,1:T(8,128)} %param.9) | data formatting | bytes 1228800 | tf_op args[2]
  9.6 0.0 copy-done
  9.7 0.7 copy.9.lengths_ref
  10.3 86.6 %shard_map.86 = (bf16[2,1,2,64,2560]{4,3,2,1,0:T(8,128)(2,1)}, f32[2,2,8,2560]{3,2,1,0:T(8,128)}) custom-call(s32[20]{0:T(128)} %layers_ref.1, s32[2,2,1]{2,1,0:T(2,128)} %copy.9.lengths_ref, f32[20,3,2560]{2,1,0:T(4,128)} %copy.10.gains_ref, bf16[2,1,2,2,64,2560]{5,4,3,2,1,0:T(8,128)(2,1)} %queries_hbm.1, bf16[2,1,2,2,64,2560]{5,4,3,2,1,0:T(8,128)(2,1)} %keys_hbm.1, ...), custom_call_target="tpu_custom_call" | custom-call | tf_op jit(solution)/shard_map/pallas_call | solution.py:375
  97.0 0.9 slice_bitcast_fusion
  97.9 0.8 collective-permute-start
  98.7 8.1 %collective-permute-done = f32[2,8,2560]{2,1,0:T(8,128)S(1)} collective-permute-done((f32[2,8,2560]{2,1,0:T(8,128)S(1)}, f32[2,8,2560]{2,1,0:T(8,128)S(1)}, u32[]{:S(2)}, u32[]{:S(2)}) %collective-permute-start) | collective-permute-done | bytes 163872 | tf_op jit(solution)/shard_map/ppermute | solution.py:408
  106.7 1.6 bitcast_add_fusion
  108.3 0.0 all-reduce.2.cloned.1.call-update
  108.4 70.5 %all-reduce.2.cloned.1.call-done = f32[2,8,2560]{2,1,0:T(8,128)} async-done(((f32[2,8,2560]{2,1,0:T(8,128)}), f32[2,8,2560]{2,1,0:T(8,128)}) %all-reduce.2.cloned.1.call-update) | async-done | bytes 163856 | tf_op jit(solution)/shard_map/psum | solution.py:411
  178.9 0.9 fusion
  179.8 0.7 copy.11
  180.5 2.5 %copy.14 = bf16[2,1,2,64,2560]{4,3,2,1,0:T(8,128)(2,1)} copy(bf16[2,1,2,64,2560]{4,3,2,1,0:T(8,128)(2,1)} %get-tuple-element.10) | data formatting | bytes 2621440
Async XLA Ops:
  7.2 2.5 %copy-start = (s32[2,2,1]{1,2,0:T(1,128)S(1)}, s32[2,2,1]{1,2,0:T(1,128)}, u32[]{:S(2)}) copy-start(s32[2,2,1]{1,2,0:T(1,128)} %param.8) | copy-start | bytes 52
  7.2 171.7 %all-reduce.2.cloned.1.call-start = ((), (), s32[]{:S(2)}) async-start(), calls=%async_computation | async-start | bytes 327680 | tf_op jit(solution)/shard_map/psum | solution.py:411
  97.9 8.8 %collective-permute-start = (f32[2,8,2560]{2,1,0:T(8,128)S(1)}, f32[2,8,2560]{2,1,0:T(8,128)S(1)}, u32[]{:S(2)}, u32[]{:S(2)}) collective-permute-start(f32[2,8,2560]{2,1,0:T(8,128)S(1)} %slice_bitcast_fusion), channel_id=1, source_target_pairs={{0,120},{8,112},{16,104},{24,96},{32,88},{40,80},{48,72},{56,64},{... | collective-permute-start | bytes 491528 | tf_op jit(solution)/shard_map/ppermute | solution.py:408
Sparse Core Ops, SparseCore 0:
  108.5 70.3 all-reduce.1

commit v2 on v1

--- a/solution.py
+++ b/solution.py
@@ -33,13 +33,18 @@
     sections,
     layers_ref,
     lengths_ref,
-    gains_ref,
+    gains_hbm,
     queries_hbm,
     keys_hbm,
     inputs_hbm,
     cotangents_hbm,
     grads_hbm,
+    sums_ref,
+    gains_ref,
     terms_ref,
+    sent_terms,
+    met_terms,
+    final_terms,
     q_buf,
     k_buf,
     h_buf,
@@ -59,8 +64,16 @@
     set_send,
     set_recv,
     out_sems,
+    gain_sem,
+    scatter_send,
+    scatter_recv,
+    gather_send,
+    gather_recv,
 ):
     place = lax.axis_index("section")
+    group = lax.axis_index("dp")
+    groups = scatter_recv.shape[1]
+    reducers = gather_recv.shape[0]
     core = lax.rem(place, 2)
     chip = lax.div(place, 2)
     chips = sections // 2
@@ -68,6 +81,7 @@
     width = q_buf.shape[4]
     pairs = width // PAIR
     layer_total = layers_ref.shape[0]
+    chunk = width // reducers
     scale = 1.0 / math.sqrt(HEAD_DIM)
     partner = {"section": place + 1 - 2 * core}
     first_direction = jnp.where(chip >= chips // 2, 0, 1)
@@ -83,6 +97,22 @@
     @pl.when(chip < chips - 1)
     def _():
         pl.semaphore_signal(barrier, inc=1, device_id={"section": place + 2}, device_id_type=MESH)
+
+    for other in range(groups):
+
+        @pl.when(other != group)
+        def _():
+            pl.semaphore_signal(barrier, inc=1, device_id={"dp": jnp.int32(other)}, device_id_type=MESH)
+
+        pl.semaphore_signal(
+            barrier,
+            inc=1,
+            device_id={"section": sections - 1 - place, "dp": jnp.int32(other)},
+            device_id_type=MESH,
+        )
+
+    gain_load = pltpu.make_async_copy(gains_hbm, gains_ref, gain_sem)
+    gain_load.start()
 
     def loads(d, m):
         copies = [pltpu.make_async_copy(inputs_hbm.at[d, 0, m], h_buf.at[d, m, 0], load_sems.at[d, m, 0])]
@@ -113,6 +143,8 @@
             def _():
                 seed(d).start()
 
+    gain_load.wait()
+
     for d in range(2):
         for whose in range(2):
             at = place if whose == 0 else place + 1 - 2 * core
@@ -122,9 +154,12 @@
                 before = before + jnp.where(layers_ref[layer] < block, 1, 0)
             for slot in range(2):
                 layer = jnp.minimum(before + slot, layer_total - 1)
-                g_buf[d, whose, slot, 0:3, :] = gains_ref[layer]
+                for row in range(3):
+                    g_buf[d, whose, slot, row : row + 1, :] = gains_ref[row, pl.ds(layer, 1), :]
 
     terms_ref[...] = jnp.zeros_like(terms_ref)
+    sent_terms[...] = jnp.zeros_like(sent_terms)
+    met_terms[0, group] = jnp.zeros((8, chunk), F32)
 
     def second_layer(d):
         block = jnp.where(d == 0, place, sections - 1 - place)
@@ -134,7 +169,7 @@
         return count == 2
 
     neighbours = 1 + jnp.where(chip > 0, 1, 0) + jnp.where(chip < chips - 1, 1, 0)
-    pl.semaphore_wait(barrier, neighbours)
+    neighbours = neighbours + 2 * groups - 1
 
     def operand_copies(d):
         mine = 1 - core
@@ -190,7 +225,7 @@
     def lane_spread(column):
         return jnp.broadcast_to(column, (seq, HEAD_DIM))
 
-    def prepare(d):
+    def prepare(d, t):
         two = second_layer(d)
 
         @pl.loop(0, 2)
@@ -198,7 +233,7 @@
             m = jnp.where(turn == 0, 1 - core, core)
             for copy in loads(d, m):
                 copy.wait()
-            length = lengths_ref[d, m, 0]
+            length = lengths_ref[d, 0, m]
             key_at = lax.broadcasted_iota(jnp.int32, (seq, 2 * seq), 0)
             query_at = lax.rem(lax.broadcasted_iota(jnp.int32, (seq, 2 * seq), 1), seq)
             allowed = (key_at <= query_at) & (key_at < length)
@@ -233,6 +268,10 @@
                     mixed = jnp.concatenate([mixed[:seq, :HEAD_DIM], mixed[seq:, HEAD_DIM:]], axis=1)
                     h_buf[d, m, slot + 1, :, cols] = (state + mixed).astype(BF16)
 
+            @pl.when((turn == 0) & (t == 0))
+            def _():
+                pl.semaphore_wait(barrier, neighbours)
+
             @pl.when(turn == 0)
             def _():
                 for copy in operand_copies(d):
@@ -244,7 +283,7 @@
         @pl.when(leading)
         def _():
             seed(d).wait()
-            length = lengths_ref[d, core, 0]
+            length = lengths_ref[d, 0, core]
             rows = lax.broadcasted_iota(jnp.int32, (seq, PAIR), 0)
             for pair in range(pairs):
                 cols = slice(pair * PAIR, (pair + 1) * PAIR)
@@ -326,6 +365,38 @@
                     terms_ref[d, slot, 1:2, cols] += shared * g_buf[d, 0, slot, 2:3, cols]
                     terms_ref[d, slot, 2:3, cols] += shared * g_buf[d, 0, slot, 1:2, cols]
 
+    def scatter_copy(d, reducer, source):
+        target = jnp.where(d == 0, place, sections - 1 - place)
+        return pltpu.make_async_remote_copy(
+            src_ref=sent_terms.at[d, :, reducer * chunk : (reducer + 1) * chunk],
+            dst_ref=met_terms.at[d, source],
+            send_sem=scatter_send.at[d, reducer],
+            recv_sem=scatter_recv.at[d, source],
+            device_id={"section": target, "dp": jnp.int32(reducer)},
+            device_id_type=MESH,
+        )
+
+    def gather_copy(reducer, target):
+        return pltpu.make_async_remote_copy(
+            src_ref=final_terms.at[reducer],
+            dst_ref=final_terms.at[reducer],
+            send_sem=gather_send.at[target],
+            recv_sem=gather_recv.at[reducer],
+            device_id={"dp": jnp.int32(target)},
+            device_id_type=MESH,
+        )
+
+    def scatter(d):
+        for slot in range(2):
+            for row in range(3):
+                at = 3 * slot + row
+                sent_terms[d, at : at + 1, :] = terms_ref[d, slot, row : row + 1, :]
+        for reducer in range(reducers):
+
+            @pl.when((d == 1) | (reducer != group))
+            def _():
+                scatter_copy(d, reducer, group).start()
+
     early = leads & (core == 0)
 
     @pl.loop(0, 6)
@@ -336,6 +407,10 @@
         late = (t >= 4) | ((t >= 1) & (t <= 2) & (t != chain_first))
         d = jnp.where(late, 1 - first_direction, first_direction)
 
+        @pl.when(jnp.logical_not(is_chain | is_terms))
+        def _():
+            prepare(d, t)
+
         @pl.when(is_chain)
         def _():
             chain(d)
@@ -343,10 +418,53 @@
         @pl.when(is_terms)
         def _():
             gain_terms(d)
-
-        @pl.when(jnp.logical_not(is_chain | is_terms))
-        def _():
-            prepare(d)
+            scatter(d)
+
+    @pl.when(group < reducers)
+    def _():
+        total = sent_terms[0, :, pl.ds(pl.multiple_of(group * chunk, chunk), chunk)]
+        for other in range(groups):
+            scatter_copy(1, 0, other).wait_recv()
+            total = total + met_terms[1, other]
+        for other in range(groups):
+
+            @pl.when(other != group)
+            def _():
+                scatter_copy(0, 0, other).wait_recv()
+
+        for other in range(groups):
+            total = total + jnp.where(other == group, 0.0, met_terms[0, other])
+        final_terms[group] = total * (1.0 / groups)
+        for other in range(groups):
+
+            @pl.when(other != group)
+            def _():
+                gather_copy(group, other).start()
+
+    for reducer in range(reducers):
+
+        @pl.when(reducer != group)
+        def _():
+            gather_copy(reducer, 0).wait_recv()
+
+        for slot in range(2):
+            for row in range(3):
+                sums_ref[0, row, slot : slot + 1, reducer * chunk : (reducer + 1) * chunk] = final_terms[
+                    reducer, 3 * slot + row : 3 * slot + row + 1, :
+                ]
+
+    for other in range(groups):
+
+        @pl.when((group < reducers) & (other != group))
+        def _():
+            gather_copy(group, other).wait_send()
+
+    for reducer in range(reducers):
+        scatter_copy(1, reducer, group).wait_send()
+
+        @pl.when(reducer != group)
+        def _():
+            scatter_copy(0, reducer, group).wait_send()
 
     for d in range(2):
         for copy in operand_copies(d):
@@ -372,15 +490,21 @@
     scalars = pl.BlockSpec(memory_space=pltpu.SMEM)
     vector = pl.BlockSpec(memory_space=pltpu.VMEM)
     dma = pltpu.SemaphoreType.DMA
-    input_grads, terms = pl.pallas_call(
+    reducers = 5
+    input_grads, sums = pl.pallas_call(
         functools.partial(kernel, sections),
         out_shape=(
             jax.ShapeDtypeStruct(block_inputs.shape, BF16),
-            jax.ShapeDtypeStruct((2, 2, 8, width), F32),
+            jax.ShapeDtypeStruct((1, 3, 2, width), F32),
         ),
-        in_specs=[scalars, scalars, vector, anywhere, anywhere, anywhere, anywhere],
+        in_specs=[scalars, scalars, anywhere, anywhere, anywhere, anywhere, anywhere],
         out_specs=(anywhere, vector),
         scratch_shapes=[
+            pltpu.VMEM((3, layer_gains.shape[0], width), F32),
+            pltpu.VMEM((2, 2, 8, width), F32),
+            pltpu.VMEM((2, 8, width), F32),
+            pltpu.VMEM((2, groups, 8, width // reducers), F32),
+            pltpu.VMEM((reducers, 8, width // reducers), F32),
             pltpu.VMEM((2, 2, 2, seq, width), BF16),
             pltpu.VMEM((2, 2, 2, seq, width), BF16),
             pltpu.VMEM((2, 3, 3, seq, width), BF16),
@@ -400,17 +524,25 @@
             dma((2,)),
             dma((2,)),
             dma((2, 2)),
+            dma,
+            dma((2, reducers)),
+            dma((2, groups)),
+            dma((groups,)),
+            dma((reducers,)),
         ],
         compiler_params=pltpu.CompilerParams(
             collective_id=0, has_side_effects=True, vmem_limit_bytes=60000 * 1024
         ),
-    )(section_of_layer, lengths, layer_gains, saved_queries, saved_keys, block_inputs, cotangents)
-    mirrored = lax.ppermute(
-        terms[1], "section", [(at, sections - 1 - at) for at in range(sections)]
+    )(
+        section_of_layer,
+        jnp.transpose(lengths, (0, 2, 1)),
+        jnp.transpose(layer_gains, (1, 0, 2)),
+        saved_queries,
+        saved_keys,
+        block_inputs,
+        cotangents,
     )
-    own_rows = lax.psum(terms[0] + mirrored, "dp")
-    gain_grads = (own_rows[:, 0:3] / groups)[None]
-    return (input_grads, gain_grads)
+    return (input_grads, jnp.transpose(sums, (0, 2, 1, 3)))
 
 
 def solution(mesh):

time: 190 us -> 104 us (0.55)
  waiting for transfers between devices: 78.6 us -> 0 us
  between operations: 14.1 us -> 0.65 us
  Pallas kernels: 86.6 us -> 100 us
  local copies, waits for them, and re-layouts: 7.14 us -> 3.1 us
  other arithmetic: 2.54 us -> 0 us
    psum x1 -> x0, waiting for transfers between devices: 70.5 us -> none  [body(): own_rows = lax.psum(terms[0] + mirrored, 'dp')]
    pallas_call x1, Pallas kernels: 86.6 us -> 100 us  [body(): pl.pallas_call(functools.partial(kernel, sections), out_shape=(jax.ShapeD...]
    ppermute x1 -> x0, waiting for transfers between devices: 8.07 us -> none  [body(): lax.ppermute(terms[1], 'section', [(at, sections - 1 - at) for at in rang...]
    unnamed x6 -> x4, local copies, waits for them, and re-layouts: 6.22 us -> 3.1 us
  transfers between devices with their start and end apart: 2 -> 0, of which waited for: 2 -> 0; matrix products, arithmetic and copies ran while one was open for 0% -> 0% of each run, Pallas kernels for 0% -> 0%
where the time goes in v2:
time: 104 us
  Pallas kernels  100 us (96%)
  local copies, waits for them, and re-layouts  3.1 us (3%)
    pallas_call x1, Pallas kernels, body(): pl.pallas_call(functools.partial(kernel, sections), out_shape=(jax.ShapeD...  100 us
    unnamed x4, local copies, waits for them, and re-layouts  3.1 us

profile of v2, /device:TPU:0, one launch (start us, length us, event | category | flops | bytes accessed | tf_op | source)
XLA Modules:
  0.0 104.0 jit_solution(13581410717293171278)
XLA Ops:
  0.6 100.2 %shard_map.86 = (bf16[2,1,2,64,2560]{4,3,2,1,0:T(8,128)(2,1)}, f32[1,3,2,2560]{3,2,1,0:T(2,128)}) custom-call(s32[20]{0:T(128)} %layers_ref.1, s32[2,1,2]{2,1,0:T(1,128)} %bitcast.7, f32[3,20,2560]{2,1,0:T(8,128)} %bitcast.5, bf16[2,1,2,2,64,2560]{5,4,3,2,1,0:T(8,128)(2,1)} %queries_hbm.1, bf16[2,1,2,2,64,2560]{5,4,3,2,1,0:T(8,128)(2,1)} %keys_hbm.1, ...), custom_call_target="tpu_custom_call" | custom-call | tf_op jit(solution)/shard_map/pallas_call | solution.py:494
  100.9 0.0 copy-start
  100.9 2.5 %copy.12 = bf16[2,1,2,64,2560]{4,3,2,1,0:T(8,128)(2,1)} copy(bf16[2,1,2,64,2560]{4,3,2,1,0:T(8,128)(2,1)} %get-tuple-element.8) | data formatting | bytes 2621440
  103.3 0.0 copy-done
  103.3 0.6 copy.13
Async XLA Ops:
  100.9 2.5 %copy-start = (f32[1,3,2,2560]{3,2,1,0:T(2,128)S(1)}, f32[1,3,2,2560]{3,2,1,0:T(2,128)}, u32[]{:S(2)}) copy-start(f32[1,3,2,2560]{3,2,1,0:T(2,128)} %get-tuple-element.5) | copy-start | bytes 184324

commit v3 on v2

v3 whole, which is shorter than its diff:
```python
import functools
import math

import jax
import jax.numpy as jnp
from jax import lax
from jax.experimental import pallas as pl
from jax.experimental.pallas import tpu as pltpu
from jax.sharding import PartitionSpec as P

HEAD_DIM = 128
PAIR = 2 * HEAD_DIM
EPSILON = 1e-06
MESH = pl.DeviceIdType.MESH
F32 = jnp.float32
BF16 = jnp.bfloat16


def blocks_apart(pair):
    zero = jnp.zeros((pair.shape[0], HEAD_DIM), pair.dtype)
    upper = jnp.concatenate([pair[:, :HEAD_DIM], zero], axis=1)
    lower = jnp.concatenate([zero, pair[:, HEAD_DIM:]], axis=1)
    return jnp.concatenate([upper, lower], axis=0)


def dot(left, right, left_dim, right_dim):
    return lax.dot_general(
        left, right, (((left_dim,), (right_dim,)), ((), ())), preferred_element_type=F32
    )


def kernel(
    sections,
    layers_ref,
    lengths_ref,
    gains_hbm,
    queries_hbm,
    keys_hbm,
    inputs_hbm,
    cotangents_hbm,
    grads_hbm,
    sums_ref,
    gains_ref,
    terms_ref,
    sent_terms,
    met_terms,
    final_terms,
    q_buf,
    k_buf,
    h_buf,
    v_buf,
    p_wide,
    p_low,
    r_buf,
    e_buf,
    x_buf,
    g_buf,
    load_sems,
    seed_sems,
    op_send,
    op_recv,
    hop_send,
    hop_recv,
    set_send,
    set_recv,
    out_sems,
    gain_sem,
    scatter_send,
    scatter_recv,
    gather_send,
    gather_recv,
):
    place = lax.axis_index("section")
    group = lax.axis_index("dp")
    groups = scatter_recv.shape[1]
    reducers = gather_recv.shape[0]
    core = lax.rem(place, 2)
    chip = lax.div(place, 2)
    chips = sections // 2
    seq = q_buf.shape[3]
    width = q_buf.shape[4]
    pairs = width // PAIR
    layer_total = layers_ref.shape[0]
    chunk = width // reducers
    scale = 1.0 / math.sqrt(HEAD_DIM)
    partner = {"section": place + 1 - 2 * core}
    first_direction = jnp.where(chip >= chips // 2, 0, 1)
    leads = (chip == chips - 1) | (chip == 0)

    runner = core == 1
    barrier = pltpu.get_barrier_semaphore()
    pl.semaphore_signal(barrier, inc=1, device_id=partner, device_id_type=MESH)

    @pl.when(runner & (chip > 0))
    def _():
        pl.semaphore_signal(barrier, inc=1, device_id={"section": place - 2}, device_id_type=MESH)

    @pl.when(runner & (chip < chips - 1))
    def _():
        pl.semaphore_signal(barrier, inc=1, device_id={"section": place + 2}, device_id_type=MESH)

    for other in range(groups):

        @pl.when(other != group)
        def _():
            pl.semaphore_signal(barrier, inc=1, device_id={"dp": jnp.int32(other)}, device_id_type=MESH)

        pl.semaphore_signal(
            barrier,
            inc=1,
            device_id={"section": sections - 1 - place, "dp": jnp.int32(other)},
            device_id_type=MESH,
        )

    gain_load = pltpu.make_async_copy(gains_hbm, gains_ref, gain_sem)
    gain_load.start()

    def state_load(d, m):
        return pltpu.make_async_copy(inputs_hbm.at[d, 0, m], h_buf.at[d, m, 0, 0], load_sems.at[d, m, 0])

    def head_loads(d, m, slot):
        return (
            pltpu.make_async_copy(
                keys_hbm.at[d, 0, slot, m], k_buf.at[d, m, slot], load_sems.at[d, m, 1 + 2 * slot]
            ),
            pltpu.make_async_copy(
                queries_hbm.at[d, 0, slot, m], q_buf.at[d, m, slot], load_sems.at[d, m, 2 + 2 * slot]
            ),
        )

    def seed(d, m):
        return pltpu.make_async_copy(cotangents_hbm.at[d, m], e_buf.at[d, m, 0], seed_sems.at[d, m])

    for phase in range(2):
        d = first_direction if phase == 0 else 1 - first_direction
        for m in range(2):
            state_load(d, m).start()
            for slot in range(2):
                for copy in head_loads(d, m, slot):
                    copy.start()
            if phase == 0:

                @pl.when(leads & runner)
                def _():
                    seed(d, m).start()

    gain_load.wait()

    for d in range(2):
        for whose in range(2):
            at = place if whose == 0 else place + 1 - 2 * core
            block = at if d == 0 else sections - 1 - at
            before = jnp.int32(0)
            for layer in range(layer_total):
                before = before + jnp.where(layers_ref[layer] < block, 1, 0)
            for slot in range(2):
                layer = jnp.minimum(before + slot, layer_total - 1)
                for row in range(3):
                    g_buf[d, whose, slot, row : row + 1, :] = gains_ref[row, pl.ds(layer, 1), :]

    terms_ref[...] = jnp.zeros_like(terms_ref)
    sent_terms[...] = jnp.zeros_like(sent_terms)
    met_terms[0, group] = jnp.zeros((8, chunk), F32)

    def second_layer(d):
        block = jnp.where(d == 0, place, sections - 1 - place)
        count = jnp.int32(0)
        for layer in range(layer_total):
            count = count + jnp.where(layers_ref[layer] == block, 1, 0)
        return count == 2

    neighbours = 1 + core * (jnp.where(chip > 0, 1, 0) + jnp.where(chip < chips - 1, 1, 0))
    neighbours = neighbours + 2 * groups - 1

    def operand_copies(d, m):
        pieces = (
            (p_low.at[d, m, 0], p_low.at[d, m, 1]),
            (h_buf.at[d, m, 0, 0:2], h_buf.at[d, m, 1, 0:2]),
            (r_buf.at[d, m, 0], r_buf.at[d, m, 1]),
        )
        return [
            pltpu.make_async_remote_copy(
                src_ref=source,
                dst_ref=target,
                send_sem=op_send.at[d, m, at],
                recv_sem=op_recv.at[d, m, at],
                device_id=partner,
                device_id_type=MESH,
            )
            for at, (source, target) in enumerate(pieces)
        ]

    def hop(d, m):
        step = jnp.where(d == 0, -2, 2)
        return pltpu.make_async_remote_copy(
            src_ref=e_buf.at[d, m, 4],
            dst_ref=e_buf.at[d, m, 0],
            send_sem=hop_send.at[d, m],
            recv_sem=hop_recv.at[d, m],
            device_id={"section": place + step},
            device_id_type=MESH,
        )

    def stage_copy(d, m, at):
        return pltpu.make_async_remote_copy(
            src_ref=e_buf.at[d, m, 2 - 2 * d + at],
            dst_ref=e_buf.at[d, m, at],
            send_sem=set_send.at[d, m, at],
            recv_sem=set_recv.at[d, m, at],
            device_id=partner,
            device_id_type=MESH,
        )

    def own_base(d):
        return core * 2 * d

    def out_copy(d, m):
        return pltpu.make_async_copy(e_buf.at[d, m, own_base(d) + 2], grads_hbm.at[d, 0, m], out_sems.at[d, m])

    def lane_spread(column):
        return jnp.broadcast_to(column, (seq, HEAD_DIM))

    def prepare(d, m, t):
        two = second_layer(d)
        state_load(d, m).wait()
        length = lengths_ref[d, 0, m]
        key_at = lax.broadcasted_iota(jnp.int32, (seq, 2 * seq), 0)
        query_at = lax.rem(lax.broadcasted_iota(jnp.int32, (seq, 2 * seq), 1), seq)
        allowed = (key_at <= query_at) & (key_at < length)

        @pl.loop(0, 2)
        def _(slot):
            for copy in head_loads(d, m, slot):
                copy.wait()
            squares = jnp.zeros((seq, HEAD_DIM), F32)
            for tile in range(width // HEAD_DIM):
                part = h_buf[d, m, 0, slot, :, tile * HEAD_DIM : (tile + 1) * HEAD_DIM].astype(F32)
                squares = squares + part * part
            inverse = lax.rsqrt(jnp.sum(squares, axis=1, keepdims=True) * (1.0 / width) + EPSILON)
            spread = lane_spread(inverse)
            spread_two = jnp.concatenate([spread, spread], axis=1)
            present = (slot == 0) | two
            r_buf[d, m, 0, slot] = jnp.where(present, spread, 0.0)
            for pair in range(pairs):
                cols = slice(pair * PAIR, (pair + 1) * PAIR)
                state = h_buf[d, m, 0, slot, :, cols].astype(F32)
                values = (state * spread_two * g_buf[d, 0, slot, 0:1, cols]).astype(BF16)
                v_buf[d, m, slot, :, cols] = values
                scaled_q = (q_buf[d, m, slot, :, cols].astype(F32) * g_buf[d, 0, slot, 1:2, cols]).astype(BF16)
                scaled_k = (k_buf[d, m, slot, :, cols].astype(F32) * g_buf[d, 0, slot, 2:3, cols]).astype(BF16)
                scores = dot(scaled_k, blocks_apart(scaled_q), 1, 1) * scale
                masked = jnp.where(allowed, scores, -1e30)
                top = jnp.max(masked, axis=0, keepdims=True)
                terms = jnp.where(allowed, jnp.exp(masked - top), 0.0)
                probs = terms * (1.0 / jnp.sum(terms, axis=0, keepdims=True))
                low = probs.astype(BF16)
                p_wide[d, m, slot, pair] = probs
                p_low[d, m, 0, slot, pair] = low
                mixed = dot(low, values, 0, 0)
                mixed = jnp.concatenate([mixed[:seq, :HEAD_DIM], mixed[seq:, HEAD_DIM:]], axis=1)
                h_buf[d, m, 0, slot + 1, :, cols] = (state + mixed).astype(BF16)

        @pl.when(t == 0)
        def _():
            pl.semaphore_wait(barrier, neighbours)

        @pl.when(core == 0)
        def _():
            for copy in operand_copies(d, m):
                copy.start()

    def chain(d, m):
        leading = jnp.where(d == 0, chip == chips - 1, chip == 0)

        @pl.when(leading)
        def _():
            seed(d, m).wait()
            length = lengths_ref[d, 0, m]
            sequence_at = lax.broadcasted_iota(jnp.int32, (seq, PAIR), 0)
            for pair in range(pairs):
                cols = slice(pair * PAIR, (pair + 1) * PAIR)
                drawn = e_buf[d, m, 0, :, cols].astype(F32)
                e_buf[d, m, 0, :, cols] = jnp.where(sequence_at < length, drawn, 0.0).astype(BF16)

        for copy in operand_copies(d, m):
            copy.wait_recv()

        @pl.when(jnp.logical_not(leading))
        def _():
            hop(d, m).wait_recv()

        @pl.loop(0, 4)
        def _(step):
            at = step - (2 - 2 * d)

            @pl.when((at >= 0) & (at <= 2))
            def _():
                stage_copy(d, m, at).start()

            whose = jnp.where(lax.div(step, 2) == d, 0, 1)
            slot = 1 - lax.rem(step, 2)
            total = jnp.zeros((seq, HEAD_DIM), F32)
            for pair in range(pairs):
                cols = slice(pair * PAIR, (pair + 1) * PAIR)
                grad = e_buf[d, m, step, :, cols]
                product = dot(p_low[d, m, whose, slot, pair], blocks_apart(grad), 1, 0)
                product = product * g_buf[d, whose, slot, 0:1, cols]
                x_buf[:, cols] = product
                weighed = product * h_buf[d, m, whose, slot, :, cols].astype(F32)
                total = total + (weighed[:, :HEAD_DIM] + weighed[:, HEAD_DIM:])
            inverse = r_buf[d, m, whose, slot]
            shift = lane_spread(jnp.sum(total, axis=1, keepdims=True) * (1.0 / width))
            shift = shift * inverse * inverse * inverse
            for tile in range(width // HEAD_DIM):
                cols = slice(tile * HEAD_DIM, (tile + 1) * HEAD_DIM)
                state = h_buf[d, m, whose, slot, :, cols].astype(F32)
                grad = e_buf[d, m, step, :, cols].astype(F32)
                e_buf[d, m, step + 1, :, cols] = (grad + (inverse * x_buf[:, cols] - state * shift)).astype(BF16)

        ending = jnp.where(d == 0, chip == 0, chip == chips - 1)

        @pl.when(jnp.logical_not(ending))
        def _():
            hop(d, m).start()

        @pl.when(d == 0)
        def _():
            stage_copy(d, m, 2).start()

    def gain_terms(d, m):
        two = second_layer(d)

        @pl.when(core == 0)
        def _():
            for at in range(3):
                stage_copy(d, m, at).wait_recv()

        out_copy(d, m).start()

        @pl.loop(0, 2)
        def _(slot):
            at = own_base(d) + 1 - slot
            inverse = r_buf[d, m, 0, slot]
            inverse_two = jnp.concatenate([inverse, inverse], axis=1)
            for pair in range(pairs):
                cols = slice(pair * PAIR, (pair + 1) * PAIR)
                grad = blocks_apart(e_buf[d, m, at, :, cols])
                value_grad = dot(p_low[d, m, 0, slot, pair], grad, 1, 0)
                normed = h_buf[d, m, 0, slot, :, cols].astype(F32) * inverse_two
                norm_term = jnp.sum(value_grad * normed, axis=0, keepdims=True)
                probs_grad = dot(v_buf[d, m, slot, :, cols], grad, 1, 1)
                probs = p_wide[d, m, slot, pair]
                delta = jnp.sum(probs * probs_grad, axis=0, keepdims=True)
                score_grad = (probs * (probs_grad - delta) * scale).astype(BF16)
                met = dot(score_grad, blocks_apart(q_buf[d, m, slot, :, cols]), 1, 0)
                shared = jnp.sum(met * k_buf[d, m, slot, :, cols].astype(F32), axis=0, keepdims=True)
                shared = jnp.where((slot == 0) | two, shared, 0.0)
                terms_ref[d, slot, 0:1, cols] += norm_term
                terms_ref[d, slot, 1:2, cols] += shared * g_buf[d, 0, slot, 2:3, cols]
                terms_ref[d, slot, 2:3, cols] += shared * g_buf[d, 0, slot, 1:2, cols]

    def scatter_copy(d, reducer, source):
        target = jnp.where(d == 0, place, sections - 1 - place)
        return pltpu.make_async_remote_copy(
            src_ref=sent_terms.at[d, :, reducer * chunk : (reducer + 1) * chunk],
            dst_ref=met_terms.at[d, source],
            send_sem=scatter_send.at[d, reducer],
            recv_sem=scatter_recv.at[d, source],
            device_id={"section": target, "dp": jnp.int32(reducer)},
            device_id_type=MESH,
        )

    def gather_copy(reducer, target):
        return pltpu.make_async_remote_copy(
            src_ref=final_terms.at[reducer],
            dst_ref=final_terms.at[reducer],
            send_sem=gather_send.at[target],
            recv_sem=gather_recv.at[reducer],
            device_id={"dp": jnp.int32(target)},
            device_id_type=MESH,
        )

    def scatter(d):
        for slot in range(2):
            for row in range(3):
                at = 3 * slot + row
                sent_terms[d, at : at + 1, :] = terms_ref[d, slot, row : row + 1, :]
        for reducer in range(reducers):

            @pl.when((d == 1) | (reducer != group))
            def _():
                scatter_copy(d, reducer, group).start()

    @pl.loop(0, 12)
    def _(t):
        later = lax.div(t - 4, 2)
        lead_unit = jnp.where(t < 4, lax.div(t, 2), jnp.where(t < 6, t - 2, jnp.where(t < 8, t - 6, later)))
        unit = jnp.where(leads, lead_unit, jnp.where(t < 4, t, later))
        odd = lax.rem(t, 2) == 1
        lead_chain = jnp.where(t < 4, odd, (t >= 8) & jnp.logical_not(odd))
        lead_terms = jnp.where(t < 8, t >= 6, odd)
        is_chain = jnp.where(leads, lead_chain, (t >= 4) & jnp.logical_not(odd))
        is_terms = jnp.where(leads, lead_terms, (t >= 4) & odd)
        d = jnp.where(unit < 2, first_direction, 1 - first_direction)
        m = lax.rem(unit, 2)

        @pl.when(jnp.logical_not(is_chain | is_terms))
        def _():
            prepare(d, m, t)

        @pl.when(is_chain & runner)
        def _():
            chain(d, m)

        @pl.when(is_terms)
        def _():
            gain_terms(d, m)

        @pl.when(is_terms & (m == 1))
        def _():
            scatter(d)

    @pl.when(group < reducers)
    def _():
        total = sent_terms[0, :, pl.ds(pl.multiple_of(group * chunk, chunk), chunk)]
        for other in range(groups):
            scatter_copy(1, 0, other).wait_recv()
            total = total + met_terms[1, other]
        for other in range(groups):

            @pl.when(other != group)
            def _():
                scatter_copy(0, 0, other).wait_recv()

        for other in range(groups):
            total = total + jnp.where(other == group, 0.0, met_terms[0, other])
        final_terms[group] = total * (1.0 / groups)
        for other in range(groups):

            @pl.when(other != group)
            def _():
                gather_copy(group, other).start()

    for reducer in range(reducers):

        @pl.when(reducer != group)
        def _():
            gather_copy(reducer, 0).wait_recv()

        for slot in range(2):
            for row in range(3):
                sums_ref[0, row, slot : slot + 1, reducer * chunk : (reducer + 1) * chunk] = final_terms[
                    reducer, 3 * slot + row : 3 * slot + row + 1, :
                ]

    for other in range(groups):

        @pl.when((group < reducers) & (other != group))
        def _():
            gather_copy(group, other).wait_send()

    for reducer in range(reducers):
        scatter_copy(1, reducer, group).wait_send()

        @pl.when(reducer != group)
        def _():
            scatter_copy(0, reducer, group).wait_send()

    for d in range(2):
        ending = (chip == 0) if d == 0 else (chip == chips - 1)
        for m in range(2):
            out_copy(d, m).wait()

            @pl.when(core == 0)
            def _():
                for copy in operand_copies(d, m):
                    copy.wait_send()

            @pl.when(runner)
            def _():
                for at in range(3):
                    stage_copy(d, m, at).wait_send()

            @pl.when(runner & jnp.logical_not(ending))
            def _():
                hop(d, m).wait_send()


def body(
    section_of_layer, lengths, layer_gains, saved_queries, saved_keys, block_inputs, cotangents
):
    sections = lax.axis_size("section")
    groups = lax.axis_size("dp")
    seq, width = block_inputs.shape[3:]
    pairs = width // PAIR
    anywhere = pl.BlockSpec(memory_space=pl.ANY)
    scalars = pl.BlockSpec(memory_space=pltpu.SMEM)
    vector = pl.BlockSpec(memory_space=pltpu.VMEM)
    dma = pltpu.SemaphoreType.DMA
    reducers = 5
    input_grads, sums = pl.pallas_call(
        functools.partial(kernel, sections),
        out_shape=(
            jax.ShapeDtypeStruct(block_inputs.shape, BF16),
            jax.ShapeDtypeStruct((1, 3, 2, width), F32),
        ),
        in_specs=[scalars, scalars, anywhere, anywhere, anywhere, anywhere, anywhere],
        out_specs=(anywhere, vector),
        scratch_shapes=[
            pltpu.VMEM((3, layer_gains.shape[0], width), F32),
            pltpu.VMEM((2, 2, 8, width), F32),
            pltpu.VMEM((2, 8, width), F32),
            pltpu.VMEM((2, groups, 8, width // reducers), F32),
            pltpu.VMEM((reducers, 8, width // reducers), F32),
            pltpu.VMEM((2, 2, 2, seq, width), BF16),
            pltpu.VMEM((2, 2, 2, seq, width), BF16),
            pltpu.VMEM((2, 2, 2, 3, seq, width), BF16),
            pltpu.VMEM((2, 2, 2, seq, width), BF16),
            pltpu.VMEM((2, 2, 2, pairs, seq, 2 * seq), F32),
            pltpu.VMEM((2, 2, 2, 2, pairs, seq, 2 * seq), BF16),
            pltpu.VMEM((2, 2, 2, 2, seq, HEAD_DIM), F32),
            pltpu.VMEM((2, 2, 5, seq, width), BF16),
            pltpu.VMEM((seq, width), F32),
            pltpu.VMEM((2, 2, 2, 8, width), F32),
            dma((2, 2, 5)),
            dma((2, 2)),
            dma((2, 2, 3)),
            dma((2, 2, 3)),
            dma((2, 2)),
            dma((2, 2)),
            dma((2, 2, 3)),
            dma((2, 2, 3)),
            dma((2, 2)),
            dma,
            dma((2, reducers)),
            dma((2, groups)),
            dma((groups,)),
            dma((reducers,)),
        ],
        compiler_params=pltpu.CompilerParams(
            collective_id=0, has_side_effects=True, vmem_limit_bytes=60000 * 1024
        ),
    )(
        section_of_layer,
        jnp.transpose(lengths, (0, 2, 1)),
        jnp.transpose(layer_gains, (1, 0, 2)),
        saved_queries,
        saved_keys,
        block_inputs,
        cotangents,
    )
    return (input_grads, jnp.transpose(sums, (0, 2, 1, 3)))


def solution(mesh):
    in_specs = (
        P(),
        P(None, None, "dp"),
        P(),
        P(None, "section", None, None, "dp", None),
        P(None, "section", None, None, "dp", None),
        P(None, "section", None, "dp", None),
        P(None, None, "dp", None),
    )
    out_specs = (P(None, "section", None, "dp", None), P("section", None, None, None))
    return jax.shard_map(body, mesh=mesh, in_specs=in_specs, out_specs=out_specs, check_vma=False)
```

time: 104 us -> 86.9 us (0.84); the launches traced: 104 us -> 85.7 us
  Pallas kernels: 100 us -> 82 us
    pallas_call x1, Pallas kernels: 100 us -> 82 us  [body(): pl.pallas_call(functools.partial(kernel, sections), out_shape=(jax.ShapeD...]
where the time goes in v3:
time: 86.9 us; the launch traced here: 85.7 us
  Pallas kernels  82 us (94%)
  local copies, waits for them, and re-layouts  3.1 us (4%)
    pallas_call x1, Pallas kernels, body(): pl.pallas_call(functools.partial(kernel, sections), out_shape=(jax.ShapeD...  82 us
    unnamed x4, local copies, waits for them, and re-layouts  3.1 us

profile of v3, /device:TPU:0, one launch (start us, length us, event | category | flops | bytes accessed | tf_op | source)
XLA Modules:
  0.0 85.7 jit_solution(8845226596219722727)
XLA Ops:
  0.6 82.0 %shard_map.86 = (bf16[2,1,2,64,2560]{4,3,2,1,0:T(8,128)(2,1)}, f32[1,3,2,2560]{3,2,1,0:T(2,128)}) custom-call(s32[20]{0:T(128)} %layers_ref.1, s32[2,1,2]{2,1,0:T(1,128)} %bitcast.7, f32[3,20,2560]{2,1,0:T(8,128)} %bitcast.5, bf16[2,1,2,2,64,2560]{5,4,3,2,1,0:T(8,128)(2,1)} %queries_hbm.1, bf16[2,1,2,2,64,2560]{5,4,3,2,1,0:T(8,128)(2,1)} %keys_hbm.1, ...), custom_call_target="tpu_custom_call" | custom-call | tf_op jit(solution)/shard_map/pallas_call | solution.py:501
  82.6 0.0 copy-start
  82.6 2.5 %copy.12 = bf16[2,1,2,64,2560]{4,3,2,1,0:T(8,128)(2,1)} copy(bf16[2,1,2,64,2560]{4,3,2,1,0:T(8,128)(2,1)} %get-tuple-element.8) | data formatting | bytes 2621440
  85.1 0.0 copy-done
  85.1 0.6 copy.13
Async XLA Ops:
  82.6 2.5 %copy-start = (f32[1,3,2,2560]{3,2,1,0:T(2,128)S(1)}, f32[1,3,2,2560]{3,2,1,0:T(2,128)}, u32[]{:S(2)}) copy-start(f32[1,3,2,2560]{3,2,1,0:T(2,128)} %get-tuple-element.5) | copy-start | bytes 184324

commit v4 on v3

--- a/solution.py
+++ b/solution.py
@@ -82,6 +82,8 @@
     pairs = width // PAIR
     layer_total = layers_ref.shape[0]
     chunk = width // reducers
+    blocks = hop_recv.shape[2]
+    block_rows = seq // blocks
     scale = 1.0 / math.sqrt(HEAD_DIM)
     partner = {"section": place + 1 - 2 * core}
     first_direction = jnp.where(chip >= chips // 2, 0, 1)
@@ -190,13 +192,14 @@
             for at, (source, target) in enumerate(pieces)
         ]
 
-    def hop(d, m):
+    def hop(d, m, block):
         step = jnp.where(d == 0, -2, 2)
+        low = seq - (block + 1) * block_rows
         return pltpu.make_async_remote_copy(
-            src_ref=e_buf.at[d, m, 4],
-            dst_ref=e_buf.at[d, m, 0],
-            send_sem=hop_send.at[d, m],
-            recv_sem=hop_recv.at[d, m],
+            src_ref=e_buf.at[d, m, 4, low : low + block_rows],
+            dst_ref=e_buf.at[d, m, 0, low : low + block_rows],
+            send_sem=hop_send.at[d, m, block],
+            recv_sem=hop_recv.at[d, m, block],
             device_id={"section": place + step},
             device_id_type=MESH,
         )
@@ -269,6 +272,50 @@
             for copy in operand_copies(d, m):
                 copy.start()
 
+    def chain_block(d, m, block, leading, ending):
+        low = seq - (block + 1) * block_rows
+        high = low + block_rows
+
+        @pl.when(jnp.logical_not(leading))
+        def _():
+            hop(d, m, block).wait_recv()
+
+        @pl.loop(0, 4)
+        def _(step):
+            if block == blocks - 1:
+                at = step - (2 - 2 * d)
+
+                @pl.when((at >= 0) & (at <= 2))
+                def _():
+                    stage_copy(d, m, at).start()
+
+            whose = jnp.where(lax.div(step, 2) == d, 0, 1)
+            slot = 1 - lax.rem(step, 2)
+            total = jnp.zeros((block_rows, HEAD_DIM), F32)
+            for pair in range(pairs):
+                cols = slice(pair * PAIR, (pair + 1) * PAIR)
+                grad = e_buf[d, m, step, low:seq, cols]
+                if low > 0:
+                    grad = jnp.concatenate([jnp.zeros((low, PAIR), BF16), grad], axis=0)
+                product = dot(p_low[d, m, whose, slot, pair, low:high, :], blocks_apart(grad), 1, 0)
+                product = product * g_buf[d, whose, slot, 0:1, cols]
+                x_buf[low:high, cols] = product
+                weighed = product * h_buf[d, m, whose, slot, low:high, cols].astype(F32)
+                total = total + (weighed[:, :HEAD_DIM] + weighed[:, HEAD_DIM:])
+            inverse = r_buf[d, m, whose, slot, low:high]
+            shift = jnp.sum(total, axis=1, keepdims=True) * (1.0 / width)
+            shift = jnp.broadcast_to(shift, (block_rows, HEAD_DIM)) * inverse * inverse * inverse
+            for tile in range(width // HEAD_DIM):
+                cols = slice(tile * HEAD_DIM, (tile + 1) * HEAD_DIM)
+                state = h_buf[d, m, whose, slot, low:high, cols].astype(F32)
+                grad = e_buf[d, m, step, low:high, cols].astype(F32)
+                grad = grad + (inverse * x_buf[low:high, cols] - state * shift)
+                e_buf[d, m, step + 1, low:high, cols] = grad.astype(BF16)
+
+        @pl.when(jnp.logical_not(ending))
+        def _():
+            hop(d, m, block).start()
+
     def chain(d, m):
         leading = jnp.where(d == 0, chip == chips - 1, chip == 0)
 
@@ -285,43 +332,9 @@
         for copy in operand_copies(d, m):
             copy.wait_recv()
 
-        @pl.when(jnp.logical_not(leading))
-        def _():
-            hop(d, m).wait_recv()
-
-        @pl.loop(0, 4)
-        def _(step):
-            at = step - (2 - 2 * d)
-
-            @pl.when((at >= 0) & (at <= 2))
-            def _():
-                stage_copy(d, m, at).start()
-
-            whose = jnp.where(lax.div(step, 2) == d, 0, 1)
-            slot = 1 - lax.rem(step, 2)
-            total = jnp.zeros((seq, HEAD_DIM), F32)
-            for pair in range(pairs):
-                cols = slice(pair * PAIR, (pair + 1) * PAIR)
-                grad = e_buf[d, m, step, :, cols]
-                product = dot(p_low[d, m, whose, slot, pair], blocks_apart(grad), 1, 0)
-                product = product * g_buf[d, whose, slot, 0:1, cols]
-                x_buf[:, cols] = product
-                weighed = product * h_buf[d, m, whose, slot, :, cols].astype(F32)
-                total = total + (weighed[:, :HEAD_DIM] + weighed[:, HEAD_DIM:])
-            inverse = r_buf[d, m, whose, slot]
-            shift = lane_spread(jnp.sum(total, axis=1, keepdims=True) * (1.0 / width))
-            shift = shift * inverse * inverse * inverse
-            for tile in range(width // HEAD_DIM):
-                cols = slice(tile * HEAD_DIM, (tile + 1) * HEAD_DIM)
-                state = h_buf[d, m, whose, slot, :, cols].astype(F32)
-                grad = e_buf[d, m, step, :, cols].astype(F32)
-                e_buf[d, m, step + 1, :, cols] = (grad + (inverse * x_buf[:, cols] - state * shift)).astype(BF16)
-
         ending = jnp.where(d == 0, chip == 0, chip == chips - 1)
-
-        @pl.when(jnp.logical_not(ending))
-        def _():
-            hop(d, m).start()
+        for block in range(blocks):
+            chain_block(d, m, block, leading, ending)
 
         @pl.when(d == 0)
         def _():
@@ -483,7 +496,8 @@
 
             @pl.when(runner & jnp.logical_not(ending))
             def _():
-                hop(d, m).wait_send()
+                for block in range(blocks):
+                    hop(d, m, block).wait_send()
 
 
 def body(
@@ -498,6 +512,7 @@
     vector = pl.BlockSpec(memory_space=pltpu.VMEM)
     dma = pltpu.SemaphoreType.DMA
     reducers = 5
+    row_blocks = 2
     input_grads, sums = pl.pallas_call(
         functools.partial(kernel, sections),
         out_shape=(
@@ -526,8 +541,8 @@
             dma((2, 2)),
             dma((2, 2, 3)),
             dma((2, 2, 3)),
-            dma((2, 2)),
-            dma((2, 2)),
+            dma((2, 2, row_blocks)),
+            dma((2, 2, row_blocks)),
             dma((2, 2, 3)),
             dma((2, 2, 3)),
             dma((2, 2)),

time: 86.9 us -> 78.1 us (0.90)
  Pallas kernels: 82 us -> 73.1 us
    pallas_call x1, Pallas kernels: 82 us -> 73.1 us  [body(): pl.pallas_call(functools.partial(kernel, sections), out_shape=(jax.ShapeD...]
where the time goes in v4:
time: 78.1 us; the launch traced here: 76.9 us
  Pallas kernels  73.1 us (94%)
  local copies, waits for them, and re-layouts  3.1 us (4%)
    pallas_call x1, Pallas kernels, body(): pl.pallas_call(functools.partial(kernel, sections), out_shape=(jax.ShapeD...  73.1 us
    unnamed x4, local copies, waits for them, and re-layouts  3.1 us

profile of v4, /device:TPU:0, one launch (start us, length us, event | category | flops | bytes accessed | tf_op | source)
XLA Modules:
  0.0 76.9 jit_solution(10066707485852166945)
XLA Ops:
  0.6 73.1 %shard_map.86 = (bf16[2,1,2,64,2560]{4,3,2,1,0:T(8,128)(2,1)}, f32[1,3,2,2560]{3,2,1,0:T(2,128)}) custom-call(s32[20]{0:T(128)} %layers_ref.1, s32[2,1,2]{2,1,0:T(1,128)} %bitcast.7, f32[3,20,2560]{2,1,0:T(8,128)} %bitcast.5, bf16[2,1,2,2,64,2560]{5,4,3,2,1,0:T(8,128)(2,1)} %queries_hbm.1, bf16[2,1,2,2,64,2560]{5,4,3,2,1,0:T(8,128)(2,1)} %keys_hbm.1, ...), custom_call_target="tpu_custom_call" | custom-call | tf_op jit(solution)/shard_map/pallas_call | solution.py:516
  73.7 0.0 copy-start
  73.8 2.5 %copy.12 = bf16[2,1,2,64,2560]{4,3,2,1,0:T(8,128)(2,1)} copy(bf16[2,1,2,64,2560]{4,3,2,1,0:T(8,128)(2,1)} %get-tuple-element.8) | data formatting | bytes 2621440
  76.2 0.0 copy-done
  76.2 0.6 copy.13
Async XLA Ops:
  73.7 2.5 %copy-start = (f32[1,3,2,2560]{3,2,1,0:T(2,128)S(1)}, f32[1,3,2,2560]{3,2,1,0:T(2,128)}, u32[]{:S(2)}) copy-start(f32[1,3,2,2560]{3,2,1,0:T(2,128)} %get-tuple-element.5) | copy-start | bytes 184324

commit v5 on v4

--- a/solution.py
+++ b/solution.py
@@ -47,12 +47,14 @@
     final_terms,
     q_buf,
     k_buf,
-    h_buf,
+    h_low,
+    h_high,
     v_buf,
     p_wide,
     p_low,
     r_buf,
-    e_buf,
+    e_even,
+    e_odd,
     x_buf,
     g_buf,
     load_sems,
@@ -118,7 +120,7 @@
     gain_load.start()
 
     def state_load(d, m):
-        return pltpu.make_async_copy(inputs_hbm.at[d, 0, m], h_buf.at[d, m, 0, 0], load_sems.at[d, m, 0])
+        return pltpu.make_async_copy(inputs_hbm.at[d, 0, m], h_low.at[d, m, 0], load_sems.at[d, m, 0])
 
     def head_loads(d, m, slot):
         return (
@@ -131,7 +133,7 @@
         )
 
     def seed(d, m):
-        return pltpu.make_async_copy(cotangents_hbm.at[d, m], e_buf.at[d, m, 0], seed_sems.at[d, m])
+        return pltpu.make_async_copy(cotangents_hbm.at[d, m], e_even.at[d, m, 0], seed_sems.at[d, m])
 
     for phase in range(2):
         d = first_direction if phase == 0 else 1 - first_direction
@@ -177,7 +179,8 @@
     def operand_copies(d, m):
         pieces = (
             (p_low.at[d, m, 0], p_low.at[d, m, 1]),
-            (h_buf.at[d, m, 0, 0:2], h_buf.at[d, m, 1, 0:2]),
+            (h_low.at[d, m, 0], h_low.at[d, m, 1]),
+            (h_high.at[d, m, 0], h_high.at[d, m, 1]),
             (r_buf.at[d, m, 0], r_buf.at[d, m, 1]),
         )
         return [
@@ -196,8 +199,8 @@
         step = jnp.where(d == 0, -2, 2)
         low = seq - (block + 1) * block_rows
         return pltpu.make_async_remote_copy(
-            src_ref=e_buf.at[d, m, 4, low : low + block_rows],
-            dst_ref=e_buf.at[d, m, 0, low : low + block_rows],
+            src_ref=e_even.at[d, m, 2, low : low + block_rows],
+            dst_ref=e_even.at[d, m, 0, low : low + block_rows],
             send_sem=hop_send.at[d, m, block],
             recv_sem=hop_recv.at[d, m, block],
             device_id={"section": place + step},
@@ -205,9 +208,11 @@
         )
 
     def stage_copy(d, m, at):
+        held = (e_even.at[d, m, 1 - d], e_odd.at[d, m, 1 - d], e_even.at[d, m, 2 - d])[at]
+        met = (e_even.at[d, m, 0], e_odd.at[d, m, 0], e_even.at[d, m, 1])[at]
         return pltpu.make_async_remote_copy(
-            src_ref=e_buf.at[d, m, 2 - 2 * d + at],
-            dst_ref=e_buf.at[d, m, at],
+            src_ref=held,
+            dst_ref=met,
             send_sem=set_send.at[d, m, at],
             recv_sem=set_recv.at[d, m, at],
             device_id=partner,
@@ -215,10 +220,10 @@
         )
 
     def own_base(d):
-        return core * 2 * d
+        return core * d
 
     def out_copy(d, m):
-        return pltpu.make_async_copy(e_buf.at[d, m, own_base(d) + 2], grads_hbm.at[d, 0, m], out_sems.at[d, m])
+        return pltpu.make_async_copy(e_even.at[d, m, own_base(d) + 1], grads_hbm.at[d, 0, m], out_sems.at[d, m])
 
     def lane_spread(column):
         return jnp.broadcast_to(column, (seq, HEAD_DIM))
@@ -231,22 +236,21 @@
         query_at = lax.rem(lax.broadcasted_iota(jnp.int32, (seq, 2 * seq), 1), seq)
         allowed = (key_at <= query_at) & (key_at < length)
 
-        @pl.loop(0, 2)
-        def _(slot):
+        for slot in range(2):
+            held = (h_low, h_high)[slot]
             for copy in head_loads(d, m, slot):
                 copy.wait()
             squares = jnp.zeros((seq, HEAD_DIM), F32)
             for tile in range(width // HEAD_DIM):
-                part = h_buf[d, m, 0, slot, :, tile * HEAD_DIM : (tile + 1) * HEAD_DIM].astype(F32)
+                part = held[d, m, 0, :, tile * HEAD_DIM : (tile + 1) * HEAD_DIM].astype(F32)
                 squares = squares + part * part
             inverse = lax.rsqrt(jnp.sum(squares, axis=1, keepdims=True) * (1.0 / width) + EPSILON)
             spread = lane_spread(inverse)
             spread_two = jnp.concatenate([spread, spread], axis=1)
-            present = (slot == 0) | two
-            r_buf[d, m, 0, slot] = jnp.where(present, spread, 0.0)
+            r_buf[d, m, 0, slot] = spread if slot == 0 else jnp.where(two, spread, 0.0)
             for pair in range(pairs):
                 cols = slice(pair * PAIR, (pair + 1) * PAIR)
-                state = h_buf[d, m, 0, slot, :, cols].astype(F32)
+                state = held[d, m, 0, :, cols].astype(F32)
                 values = (state * spread_two * g_buf[d, 0, slot, 0:1, cols]).astype(BF16)
                 v_buf[d, m, slot, :, cols] = values
                 scaled_q = (q_buf[d, m, slot, :, cols].astype(F32) * g_buf[d, 0, slot, 1:2, cols]).astype(BF16)
@@ -259,9 +263,10 @@
                 low = probs.astype(BF16)
                 p_wide[d, m, slot, pair] = probs
                 p_low[d, m, 0, slot, pair] = low
-                mixed = dot(low, values, 0, 0)
-                mixed = jnp.concatenate([mixed[:seq, :HEAD_DIM], mixed[seq:, HEAD_DIM:]], axis=1)
-                h_buf[d, m, 0, slot + 1, :, cols] = (state + mixed).astype(BF16)
+                if slot == 0:
+                    mixed = dot(low, values, 0, 0)
+                    mixed = jnp.concatenate([mixed[:seq, :HEAD_DIM], mixed[seq:, HEAD_DIM:]], axis=1)
+                    h_high[d, m, 0, :, cols] = (state + mixed).astype(BF16)
 
         @pl.when(t == 0)
         def _():
@@ -280,37 +285,57 @@
         def _():
             hop(d, m, block).wait_recv()
 
-        @pl.loop(0, 4)
-        def _(step):
-            if block == blocks - 1:
-                at = step - (2 - 2 * d)
-
-                @pl.when((at >= 0) & (at <= 2))
+        @pl.loop(0, 2)
+        def _(visit):
+            whose = jnp.where(visit == d, 0, 1)
+            if block == 0:
+
+                @pl.when(visit == 1 - d)
                 def _():
-                    stage_copy(d, m, at).start()
-
-            whose = jnp.where(lax.div(step, 2) == d, 0, 1)
-            slot = 1 - lax.rem(step, 2)
-            total = jnp.zeros((block_rows, HEAD_DIM), F32)
-            for pair in range(pairs):
-                cols = slice(pair * PAIR, (pair + 1) * PAIR)
-                grad = e_buf[d, m, step, low:seq, cols]
-                if low > 0:
-                    grad = jnp.concatenate([jnp.zeros((low, PAIR), BF16), grad], axis=0)
-                product = dot(p_low[d, m, whose, slot, pair, low:high, :], blocks_apart(grad), 1, 0)
-                product = product * g_buf[d, whose, slot, 0:1, cols]
-                x_buf[low:high, cols] = product
-                weighed = product * h_buf[d, m, whose, slot, low:high, cols].astype(F32)
-                total = total + (weighed[:, :HEAD_DIM] + weighed[:, HEAD_DIM:])
-            inverse = r_buf[d, m, whose, slot, low:high]
-            shift = jnp.sum(total, axis=1, keepdims=True) * (1.0 / width)
-            shift = jnp.broadcast_to(shift, (block_rows, HEAD_DIM)) * inverse * inverse * inverse
-            for tile in range(width // HEAD_DIM):
-                cols = slice(tile * HEAD_DIM, (tile + 1) * HEAD_DIM)
-                state = h_buf[d, m, whose, slot, low:high, cols].astype(F32)
-                grad = e_buf[d, m, step, low:high, cols].astype(F32)
-                grad = grad + (inverse * x_buf[low:high, cols] - state * shift)
-                e_buf[d, m, step + 1, low:high, cols] = grad.astype(BF16)
+                    for copy in operand_copies(d, m):
+                        copy.wait_recv()
+
+            for slot in (1, 0):
+                if block == blocks - 1:
+                    if slot == 1:
+
+                        @pl.when(visit == 1 - d)
+                        def _():
+                            stage_copy(d, m, 0).start()
+
+                        @pl.when(visit > 1 - d)
+                        def _():
+                            stage_copy(d, m, 2).start()
+
+                    else:
+
+                        @pl.when(visit == 1 - d)
+                        def _():
+                            stage_copy(d, m, 1).start()
+
+                before, after = (e_odd, e_even) if slot == 0 else (e_even, e_odd)
+                held = (h_low, h_high)[slot]
+                onward = visit + 1 - slot
+                total = jnp.zeros((block_rows, HEAD_DIM), F32)
+                for pair in range(pairs):
+                    cols = slice(pair * PAIR, (pair + 1) * PAIR)
+                    grad = before[d, m, visit, low:seq, cols]
+                    if low > 0:
+                        grad = jnp.concatenate([jnp.zeros((low, PAIR), BF16), grad], axis=0)
+                    product = dot(p_low[d, m, whose, slot, pair, low:high, :], blocks_apart(grad), 1, 0)
+                    product = product * g_buf[d, whose, slot, 0:1, cols]
+                    x_buf[low:high, cols] = product
+                    weighed = product * held[d, m, whose, low:high, cols].astype(F32)
+                    total = total + (weighed[:, :HEAD_DIM] + weighed[:, HEAD_DIM:])
+                inverse = r_buf[d, m, whose, slot, low:high]
+                shift = jnp.sum(total, axis=1, keepdims=True) * (1.0 / width)
+                shift = jnp.broadcast_to(shift, (block_rows, HEAD_DIM)) * inverse * inverse * inverse
+                for tile in range(width // HEAD_DIM):
+                    cols = slice(tile * HEAD_DIM, (tile + 1) * HEAD_DIM)
+                    state = held[d, m, whose, low:high, cols].astype(F32)
+                    grad = before[d, m, visit, low:high, cols].astype(F32)
+                    grad = grad + (inverse * x_buf[low:high, cols] - state * shift)
+                    after[d, m, onward, low:high, cols] = grad.astype(BF16)
 
         @pl.when(jnp.logical_not(ending))
         def _():
@@ -326,11 +351,8 @@
             sequence_at = lax.broadcasted_iota(jnp.int32, (seq, PAIR), 0)
             for pair in range(pairs):
                 cols = slice(pair * PAIR, (pair + 1) * PAIR)
-                drawn = e_buf[d, m, 0, :, cols].astype(F32)
-                e_buf[d, m, 0, :, cols] = jnp.where(sequence_at < length, drawn, 0.0).astype(BF16)
-
-        for copy in operand_copies(d, m):
-            copy.wait_recv()
+                drawn = e_even[d, m, 0, :, cols].astype(F32)
+                e_even[d, m, 0, :, cols] = jnp.where(sequence_at < length, drawn, 0.0).astype(BF16)
 
         ending = jnp.where(d == 0, chip == 0, chip == chips - 1)
         for block in range(blocks):
@@ -350,16 +372,16 @@
 
         out_copy(d, m).start()
 
-        @pl.loop(0, 2)
-        def _(slot):
-            at = own_base(d) + 1 - slot
+        for slot in range(2):
+            held = (h_low, h_high)[slot]
+            stage = (e_odd, e_even)[slot]
             inverse = r_buf[d, m, 0, slot]
             inverse_two = jnp.concatenate([inverse, inverse], axis=1)
             for pair in range(pairs):
                 cols = slice(pair * PAIR, (pair + 1) * PAIR)
-                grad = blocks_apart(e_buf[d, m, at, :, cols])
+                grad = blocks_apart(stage[d, m, own_base(d), :, cols])
                 value_grad = dot(p_low[d, m, 0, slot, pair], grad, 1, 0)
-                normed = h_buf[d, m, 0, slot, :, cols].astype(F32) * inverse_two
+                normed = held[d, m, 0, :, cols].astype(F32) * inverse_two
                 norm_term = jnp.sum(value_grad * normed, axis=0, keepdims=True)
                 probs_grad = dot(v_buf[d, m, slot, :, cols], grad, 1, 1)
                 probs = p_wide[d, m, slot, pair]
@@ -367,7 +389,7 @@
                 score_grad = (probs * (probs_grad - delta) * scale).astype(BF16)
                 met = dot(score_grad, blocks_apart(q_buf[d, m, slot, :, cols]), 1, 0)
                 shared = jnp.sum(met * k_buf[d, m, slot, :, cols].astype(F32), axis=0, keepdims=True)
-                shared = jnp.where((slot == 0) | two, shared, 0.0)
+                shared = shared if slot == 0 else jnp.where(two, shared, 0.0)
                 terms_ref[d, slot, 0:1, cols] += norm_term
                 terms_ref[d, slot, 1:2, cols] += shared * g_buf[d, 0, slot, 2:3, cols]
                 terms_ref[d, slot, 2:3, cols] += shared * g_buf[d, 0, slot, 1:2, cols]
@@ -404,16 +426,20 @@
             def _():
                 scatter_copy(d, reducer, group).start()
 
+    middle = (chip == chips // 2) | (chip == chips // 2 - 1)
+
     @pl.loop(0, 12)
     def _(t):
-        later = lax.div(t - 4, 2)
-        lead_unit = jnp.where(t < 4, lax.div(t, 2), jnp.where(t < 6, t - 2, jnp.where(t < 8, t - 6, later)))
-        unit = jnp.where(leads, lead_unit, jnp.where(t < 4, t, later))
         odd = lax.rem(t, 2) == 1
+        lead_unit = jnp.where(t < 4, lax.div(t, 2), jnp.where(t < 6, t - 2, jnp.where(t < 8, t - 6, lax.div(t - 4, 2))))
+        other_unit = 2 * lax.div(t - 4, 4) + lax.rem(t - 4, 2)
+        late_unit = jnp.where(middle, lax.rem(t, 4), other_unit)
+        unit = jnp.where(leads, lead_unit, jnp.where(t < 4, t, late_unit))
         lead_chain = jnp.where(t < 4, odd, (t >= 8) & jnp.logical_not(odd))
         lead_terms = jnp.where(t < 8, t >= 6, odd)
-        is_chain = jnp.where(leads, lead_chain, (t >= 4) & jnp.logical_not(odd))
-        is_terms = jnp.where(leads, lead_terms, (t >= 4) & odd)
+        late_terms = jnp.where(middle, t >= 8, lax.rem(t, 4) >= 2)
+        is_chain = jnp.where(leads, lead_chain, (t >= 4) & jnp.logical_not(late_terms))
+        is_terms = jnp.where(leads, lead_terms, (t >= 4) & late_terms)
         d = jnp.where(unit < 2, first_direction, 1 - first_direction)
         m = lax.rem(unit, 2)
 
@@ -529,18 +555,20 @@
             pltpu.VMEM((reducers, 8, width // reducers), F32),
             pltpu.VMEM((2, 2, 2, seq, width), BF16),
             pltpu.VMEM((2, 2, 2, seq, width), BF16),
-            pltpu.VMEM((2, 2, 2, 3, seq, width), BF16),
+            pltpu.VMEM((2, 2, 2, seq, width), BF16),
+            pltpu.VMEM((2, 2, 2, seq, width), BF16),
             pltpu.VMEM((2, 2, 2, seq, width), BF16),
             pltpu.VMEM((2, 2, 2, pairs, seq, 2 * seq), F32),
             pltpu.VMEM((2, 2, 2, 2, pairs, seq, 2 * seq), BF16),
             pltpu.VMEM((2, 2, 2, 2, seq, HEAD_DIM), F32),
-            pltpu.VMEM((2, 2, 5, seq, width), BF16),
+            pltpu.VMEM((2, 2, 3, seq, width), BF16),
+            pltpu.VMEM((2, 2, 2, seq, width), BF16),
             pltpu.VMEM((seq, width), F32),
             pltpu.VMEM((2, 2, 2, 8, width), F32),
             dma((2, 2, 5)),
             dma((2, 2)),
-            dma((2, 2, 3)),
-            dma((2, 2, 3)),
+            dma((2, 2, 4)),
+            dma((2, 2, 4)),
             dma((2, 2, row_blocks)),
             dma((2, 2, row_blocks)),
             dma((2, 2, 3)),

time: 78.1 us -> 74 us (0.948)
  Pallas kernels: 73.1 us -> 68.9 us
    pallas_call x1, Pallas kernels: 73.1 us -> 68.9 us  [body(): pl.pallas_call(functools.partial(kernel, sections), out_shape=(jax.ShapeD...]
where the time goes in v5:
time: 74 us; the launch traced here: 72.6 us
  Pallas kernels  68.9 us (93%)
  local copies, waits for them, and re-layouts  3.1 us (4%)
    pallas_call x1, Pallas kernels, body(): pl.pallas_call(functools.partial(kernel, sections), out_shape=(jax.ShapeD...  68.9 us
    unnamed x4, local copies, waits for them, and re-layouts  3.1 us

profile of v5, /device:TPU:0, one launch (start us, length us, event | category | flops | bytes accessed | tf_op | source)
XLA Modules:
  0.0 72.6 jit_solution(5038568287059526113)
XLA Ops:
  0.6 68.9 %shard_map.86 = (bf16[2,1,2,64,2560]{4,3,2,1,0:T(8,128)(2,1)}, f32[1,3,2,2560]{3,2,1,0:T(2,128)}) custom-call(s32[20]{0:T(128)} %layers_ref.1, s32[2,1,2]{2,1,0:T(1,128)} %bitcast.7, f32[3,20,2560]{2,1,0:T(8,128)} %bitcast.5, bf16[2,1,2,2,64,2560]{5,4,3,2,1,0:T(8,128)(2,1)} %queries_hbm.1, bf16[2,1,2,2,64,2560]{5,4,3,2,1,0:T(8,128)(2,1)} %keys_hbm.1, ...), custom_call_target="tpu_custom_call" | custom-call | tf_op jit(solution)/shard_map/pallas_call | solution.py:542
  69.5 0.0 copy-start
  69.5 2.5 %copy.12 = bf16[2,1,2,64,2560]{4,3,2,1,0:T(8,128)(2,1)} copy(bf16[2,1,2,64,2560]{4,3,2,1,0:T(8,128)(2,1)} %get-tuple-element.8) | data formatting | bytes 2621440
  72.0 0.0 copy-done
  72.0 0.6 copy.13
Async XLA Ops:
  69.5 2.5 %copy-start = (f32[1,3,2,2560]{3,2,1,0:T(2,128)S(1)}, f32[1,3,2,2560]{3,2,1,0:T(2,128)}, u32[]{:S(2)}) copy-start(f32[1,3,2,2560]{3,2,1,0:T(2,128)} %get-tuple-element.5) | copy-start | bytes 184324

commit v6 on v5

--- a/solution.py
+++ b/solution.py
@@ -91,17 +91,28 @@
     first_direction = jnp.where(chip >= chips // 2, 0, 1)
     leads = (chip == chips - 1) | (chip == 0)
 
-    runner = core == 1
+    def runner_of(d, at):
+        middle = (at == chips // 2) | (at == chips // 2 - 1)
+        later = jnp.where(at >= chips // 2, 1, 0)
+        return jnp.where(middle & (d == later), 0, 1)
+
+    def runs(d):
+        return core == runner_of(d, chip)
+
     barrier = pltpu.get_barrier_semaphore()
     pl.semaphore_signal(barrier, inc=1, device_id=partner, device_id_type=MESH)
-
-    @pl.when(runner & (chip > 0))
-    def _():
-        pl.semaphore_signal(barrier, inc=1, device_id={"section": place - 2}, device_id_type=MESH)
-
-    @pl.when(runner & (chip < chips - 1))
-    def _():
-        pl.semaphore_signal(barrier, inc=1, device_id={"section": place + 2}, device_id_type=MESH)
+    neighbours = 2 * groups
+    for d in range(2):
+        for way in (-1, 1):
+            at = chip + way
+            linked = runs(d) & (at >= 0) & (at < chips)
+            neighbours = neighbours + jnp.where(linked, 1, 0)
+
+            @pl.when(linked)
+            def _():
+                pl.semaphore_signal(
+                    barrier, inc=1, device_id={"section": 2 * at + runner_of(d, at)}, device_id_type=MESH
+                )
 
     for other in range(groups):
 
@@ -144,7 +155,7 @@
                     copy.start()
             if phase == 0:
 
-                @pl.when(leads & runner)
+                @pl.when(leads & (core == 1))
                 def _():
                     seed(d, m).start()
 
@@ -172,9 +183,6 @@
         for layer in range(layer_total):
             count = count + jnp.where(layers_ref[layer] == block, 1, 0)
         return count == 2
-
-    neighbours = 1 + core * (jnp.where(chip > 0, 1, 0) + jnp.where(chip < chips - 1, 1, 0))
-    neighbours = neighbours + 2 * groups - 1
 
     def operand_copies(d, m):
         pieces = (
@@ -196,19 +204,23 @@
         ]
 
     def hop(d, m, block):
-        step = jnp.where(d == 0, -2, 2)
+        at = chip + jnp.where(d == 0, -1, 1)
         low = seq - (block + 1) * block_rows
         return pltpu.make_async_remote_copy(
             src_ref=e_even.at[d, m, 2, low : low + block_rows],
             dst_ref=e_even.at[d, m, 0, low : low + block_rows],
             send_sem=hop_send.at[d, m, block],
             recv_sem=hop_recv.at[d, m, block],
-            device_id={"section": place + step},
+            device_id={"section": 2 * at + runner_of(d, at)},
             device_id_type=MESH,
         )
 
+    def partner_visit(d):
+        return jnp.where(core == 1, 1 - d, d)
+
     def stage_copy(d, m, at):
-        held = (e_even.at[d, m, 1 - d], e_odd.at[d, m, 1 - d], e_even.at[d, m, 2 - d])[at]
+        visit = partner_visit(d)
+        held = (e_even.at[d, m, visit], e_odd.at[d, m, visit], e_even.at[d, m, visit + 1])[at]
         met = (e_even.at[d, m, 0], e_odd.at[d, m, 0], e_even.at[d, m, 1])[at]
         return pltpu.make_async_remote_copy(
             src_ref=held,
@@ -220,7 +232,7 @@
         )
 
     def own_base(d):
-        return core * d
+        return jnp.where(runs(d), 1 - partner_visit(d), 0)
 
     def out_copy(d, m):
         return pltpu.make_async_copy(e_even.at[d, m, own_base(d) + 1], grads_hbm.at[d, 0, m], out_sems.at[d, m])
@@ -272,7 +284,7 @@
         def _():
             pl.semaphore_wait(barrier, neighbours)
 
-        @pl.when(core == 0)
+        @pl.when(jnp.logical_not(runs(d)))
         def _():
             for copy in operand_copies(d, m):
                 copy.start()
@@ -287,10 +299,10 @@
 
         @pl.loop(0, 2)
         def _(visit):
-            whose = jnp.where(visit == d, 0, 1)
+            whose = jnp.where(visit == partner_visit(d), 1, 0)
             if block == 0:
 
-                @pl.when(visit == 1 - d)
+                @pl.when(visit == partner_visit(d))
                 def _():
                     for copy in operand_copies(d, m):
                         copy.wait_recv()
@@ -299,17 +311,17 @@
                 if block == blocks - 1:
                     if slot == 1:
 
-                        @pl.when(visit == 1 - d)
+                        @pl.when(visit == partner_visit(d))
                         def _():
                             stage_copy(d, m, 0).start()
 
-                        @pl.when(visit > 1 - d)
+                        @pl.when(visit > partner_visit(d))
                         def _():
                             stage_copy(d, m, 2).start()
 
                     else:
 
-                        @pl.when(visit == 1 - d)
+                        @pl.when(visit == partner_visit(d))
                         def _():
                             stage_copy(d, m, 1).start()
 
@@ -358,14 +370,14 @@
         for block in range(blocks):
             chain_block(d, m, block, leading, ending)
 
-        @pl.when(d == 0)
+        @pl.when(partner_visit(d) == 1)
         def _():
             stage_copy(d, m, 2).start()
 
     def gain_terms(d, m):
         two = second_layer(d)
 
-        @pl.when(core == 0)
+        @pl.when(jnp.logical_not(runs(d)))
         def _():
             for at in range(3):
                 stage_copy(d, m, at).wait_recv()
@@ -447,7 +459,7 @@
         def _():
             prepare(d, m, t)
 
-        @pl.when(is_chain & runner)
+        @pl.when(is_chain & runs(d))
         def _():
             chain(d, m)
 
@@ -510,17 +522,17 @@
         for m in range(2):
             out_copy(d, m).wait()
 
-            @pl.when(core == 0)
+            @pl.when(jnp.logical_not(runs(d)))
             def _():
                 for copy in operand_copies(d, m):
                     copy.wait_send()
 
-            @pl.when(runner)
+            @pl.when(runs(d))
             def _():
                 for at in range(3):
                     stage_copy(d, m, at).wait_send()
 
-            @pl.when(runner & jnp.logical_not(ending))
+            @pl.when(runs(d) & jnp.logical_not(ending))
             def _():
                 for block in range(blocks):
                     hop(d, m, block).wait_send()
@@ -538,7 +550,7 @@
     vector = pl.BlockSpec(memory_space=pltpu.VMEM)
     dma = pltpu.SemaphoreType.DMA
     reducers = 5
-    row_blocks = 2
+    row_blocks = 4
     input_grads, sums = pl.pallas_call(
         functools.partial(kernel, sections),
         out_shape=(

time: 74 us -> 71.2 us (0.962)
  Pallas kernels: 68.9 us -> 66.2 us
    pallas_call x1, Pallas kernels: 68.9 us -> 66.2 us  [body(): pl.pallas_call(functools.partial(kernel, sections), out_shape=(jax.ShapeD...]
where the time goes in v6:
time: 71.2 us; the launch traced here: 69.9 us
  Pallas kernels  66.2 us (93%)
  local copies, waits for them, and re-layouts  3.1 us (4%)
    pallas_call x1, Pallas kernels, body(): pl.pallas_call(functools.partial(kernel, sections), out_shape=(jax.ShapeD...  66.2 us
    unnamed x4, local copies, waits for them, and re-layouts  3.1 us

profile of v6, /device:TPU:0, one launch (start us, length us, event | category | flops | bytes accessed | tf_op | source)
XLA Modules:
  0.0 69.9 jit_solution(4994447139326117507)
XLA Ops:
  0.6 66.2 %shard_map.86 = (bf16[2,1,2,64,2560]{4,3,2,1,0:T(8,128)(2,1)}, f32[1,3,2,2560]{3,2,1,0:T(2,128)}) custom-call(s32[20]{0:T(128)} %layers_ref.1, s32[2,1,2]{2,1,0:T(1,128)} %bitcast.7, f32[3,20,2560]{2,1,0:T(8,128)} %bitcast.5, bf16[2,1,2,2,64,2560]{5,4,3,2,1,0:T(8,128)(2,1)} %queries_hbm.1, bf16[2,1,2,2,64,2560]{5,4,3,2,1,0:T(8,128)(2,1)} %keys_hbm.1, ...), custom_call_target="tpu_custom_call" | custom-call | tf_op jit(solution)/shard_map/pallas_call | solution.py:554
  66.8 0.0 copy-start
  66.8 2.5 %copy.12 = bf16[2,1,2,64,2560]{4,3,2,1,0:T(8,128)(2,1)} copy(bf16[2,1,2,64,2560]{4,3,2,1,0:T(8,128)(2,1)} %get-tuple-element.8) | data formatting | bytes 2621440
  69.3 0.0 copy-done
  69.3 0.6 copy.13
Async XLA Ops:
  66.8 2.5 %copy-start = (f32[1,3,2,2560]{3,2,1,0:T(2,128)S(1)}, f32[1,3,2,2560]{3,2,1,0:T(2,128)}, u32[]{:S(2)}) copy-start(f32[1,3,2,2560]{3,2,1,0:T(2,128)} %get-tuple-element.5) | copy-start | bytes 184324

commit v7 on v6

--- a/solution.py
+++ b/solution.py
@@ -186,10 +186,11 @@
 
     def operand_copies(d, m):
         pieces = (
-            (p_low.at[d, m, 0], p_low.at[d, m, 1]),
-            (h_low.at[d, m, 0], h_low.at[d, m, 1]),
+            (p_low.at[d, m, 0, 1], p_low.at[d, m, 1, 1]),
             (h_high.at[d, m, 0], h_high.at[d, m, 1]),
             (r_buf.at[d, m, 0], r_buf.at[d, m, 1]),
+            (p_low.at[d, m, 0, 0], p_low.at[d, m, 1, 0]),
+            (h_low.at[d, m, 0], h_low.at[d, m, 1]),
         )
         return [
             pltpu.make_async_remote_copy(
@@ -300,14 +301,14 @@
         @pl.loop(0, 2)
         def _(visit):
             whose = jnp.where(visit == partner_visit(d), 1, 0)
-            if block == 0:
-
-                @pl.when(visit == partner_visit(d))
-                def _():
-                    for copy in operand_copies(d, m):
-                        copy.wait_recv()
-
             for slot in (1, 0):
+                if block == 0:
+
+                    @pl.when(visit == partner_visit(d))
+                    def _():
+                        for copy in operand_copies(d, m)[3 - 3 * slot : 5 - 2 * slot]:
+                            copy.wait_recv()
+
                 if block == blocks - 1:
                     if slot == 1:
 
@@ -438,18 +439,18 @@
             def _():
                 scatter_copy(d, reducer, group).start()
 
-    middle = (chip == chips // 2) | (chip == chips // 2 - 1)
+    inner = (chip >= chips // 2 - 2) & (chip <= chips // 2 + 1)
 
     @pl.loop(0, 12)
     def _(t):
         odd = lax.rem(t, 2) == 1
         lead_unit = jnp.where(t < 4, lax.div(t, 2), jnp.where(t < 6, t - 2, jnp.where(t < 8, t - 6, lax.div(t - 4, 2))))
         other_unit = 2 * lax.div(t - 4, 4) + lax.rem(t - 4, 2)
-        late_unit = jnp.where(middle, lax.rem(t, 4), other_unit)
+        late_unit = jnp.where(inner, lax.rem(t, 4), other_unit)
         unit = jnp.where(leads, lead_unit, jnp.where(t < 4, t, late_unit))
         lead_chain = jnp.where(t < 4, odd, (t >= 8) & jnp.logical_not(odd))
         lead_terms = jnp.where(t < 8, t >= 6, odd)
-        late_terms = jnp.where(middle, t >= 8, lax.rem(t, 4) >= 2)
+        late_terms = jnp.where(inner, t >= 8, lax.rem(t, 4) >= 2)
         is_chain = jnp.where(leads, lead_chain, (t >= 4) & jnp.logical_not(late_terms))
         is_terms = jnp.where(leads, lead_terms, (t >= 4) & late_terms)
         d = jnp.where(unit < 2, first_direction, 1 - first_direction)
@@ -579,8 +580,8 @@
             pltpu.VMEM((2, 2, 2, 8, width), F32),
             dma((2, 2, 5)),
             dma((2, 2)),
-            dma((2, 2, 4)),
-            dma((2, 2, 4)),
+            dma((2, 2, 5)),
+            dma((2, 2, 5)),
             dma((2, 2, row_blocks)),
             dma((2, 2, row_blocks)),
             dma((2, 2, 3)),

time: 71.2 us -> 70.9 us (level)
  no operation moved by 1% of the time
where the time goes in v7:
time: 70.9 us; the launch traced here: 69.7 us
  Pallas kernels  65.9 us (93%)
  local copies, waits for them, and re-layouts  3.1 us (4%)
    pallas_call x1, Pallas kernels, body(): pl.pallas_call(functools.partial(kernel, sections), out_shape=(jax.ShapeD...  65.9 us
    unnamed x4, local copies, waits for them, and re-layouts  3.1 us

profile of v7, /device:TPU:0, one launch (start us, length us, event | category | flops | bytes accessed | tf_op | source)
XLA Modules:
  0.0 69.7 jit_solution(3474124579237823883)
XLA Ops:
  0.6 65.9 %shard_map.86 = (bf16[2,1,2,64,2560]{4,3,2,1,0:T(8,128)(2,1)}, f32[1,3,2,2560]{3,2,1,0:T(2,128)}) custom-call(s32[20]{0:T(128)} %layers_ref.1, s32[2,1,2]{2,1,0:T(1,128)} %bitcast.7, f32[3,20,2560]{2,1,0:T(8,128)} %bitcast.5, bf16[2,1,2,2,64,2560]{5,4,3,2,1,0:T(8,128)(2,1)} %queries_hbm.1, bf16[2,1,2,2,64,2560]{5,4,3,2,1,0:T(8,128)(2,1)} %keys_hbm.1, ...), custom_call_target="tpu_custom_call" | custom-call | tf_op jit(solution)/shard_map/pallas_call | solution.py:555
  66.6 0.0 copy-start
  66.6 2.5 %copy.12 = bf16[2,1,2,64,2560]{4,3,2,1,0:T(8,128)(2,1)} copy(bf16[2,1,2,64,2560]{4,3,2,1,0:T(8,128)(2,1)} %get-tuple-element.8) | data formatting | bytes 2621440
  69.0 0.0 copy-done
  69.0 0.6 copy.13
Async XLA Ops:
  66.6 2.5 %copy-start = (f32[1,3,2,2560]{3,2,1,0:T(2,128)S(1)}, f32[1,3,2,2560]{3,2,1,0:T(2,128)}, u32[]{:S(2)}) copy-start(f32[1,3,2,2560]{3,2,1,0:T(2,128)} %get-tuple-element.5) | copy-start | bytes 184324
